TPU v7x, 128 devices: a whole 4x4x4 slice. The times are simulated.
128 devices in a mesh: grp: 4 (over y_hi, core), blk: 32 (over z, x, y_lo).
Axes of the slice: x: 4, y: 4 (y_hi: 2, y_lo: 2; y = y_hi * 2 + y_lo), z: 4, core: 2. Of those that a mesh axis runs over, the one named last changes fastest.
Arguments:
- state: float32 [4, 3, 512, 4096], P('grp', None, None, 'blk'), may hold values from -1 to 1
- material: float32 [4, 3, 512, 4096], P('grp', None, None, 'blk'), may hold values from 0.5 to 2
- occupied: int32 [16384], P(('grp', 'blk')), may hold values from 0 to 1, as said below
- brick_column: int32 [16384, 1], P(('grp', 'blk')), may hold values from 0 to 31, as said below
- brick_octant: int32 [16384], P(('grp', 'blk')), may hold values from 0 to 383
Outputs:
- new_state: float32 [4, 3, 512, 4096], P('grp', None, None, 'blk')
Inputs may be any that keep to these rules, and one draw needn't show every extreme that they name: `brick_column`: the rows of one device name at most 8 elements of one column, and exactly 8 of some column; rows of grp index 3 are not read. `brick_octant`: rows of grp index 3 are not read. The slots e < 8 of every device are occupied.
All inputs are finite; a program needn't handle non-finite values.
Results may differ from a plain program's by a relative error of at most 0.00074.
Values may be sent and summed in bfloat16 or wider, within the bound.
A program may use at most 128 MiB of HBM per device.

v0:
```python
import functools

import jax
import jax.numpy as jnp
from jax import lax
from jax.experimental import pallas as pl
from jax.experimental.pallas import tpu as pltpu
from jax.sharding import PartitionSpec as P

STEPS = 2
UNIT_LENGTH = 0.02
TIME_STEP = 0.1
PENALTY = 1.0
PRESSURE_SCALE = 0.05
DILATION_SCALE = 50.0
SWEEP_STEP = 0.03
SOURCE_RATE = 2.0
CUBIC_TERM = 0.3

MESH = pl.DeviceIdType.MESH
F32 = jnp.float32
BF16 = jnp.bfloat16
LANES = 128
NODES = 512
CAP = 8
DEPTH_OCTANTS = 96
LAYER = 128


def iota(shape, dim):
    return lax.broadcasted_iota(jnp.int32, shape, dim)


def flag(mask, dtype=F32):
    return jnp.where(mask, 1.0, 0.0).astype(dtype)


def wait_all(ref, sem):
    pltpu.make_async_copy(ref, ref, sem).wait()


def rows_of(ref, start, count):
    return ref[pl.ds(pl.multiple_of(start, count), count), :]


def slab(ref, r, i):
    return rows_of(ref, r * 512 + i * 64, 64).reshape(8, 8, LANES)


def put_slab(ref, r, i, value):
    ref[pl.ds(pl.multiple_of(r * 512 + i * 64, 64), 64), :] = value.reshape(64, LANES)


def along_j(s):
    return jnp.concatenate([s[1:2] - s[0:1], 0.5 * (s[2:] - s[:-2]), s[7:8] - s[6:7]], axis=0)


def along_k(s):
    k = iota(s.shape, 1)
    edge = (k == 0) | (k == 7)
    upper = jnp.where(k == 7, s, pltpu.roll(s, 7, 1))
    lower = jnp.where(k == 0, s, pltpu.roll(s, 1, 1))
    return (upper - lower) * jnp.where(edge, 1.0, 0.5)


def i_span(i):
    below, above = jnp.maximum(i - 1, 0), jnp.minimum(i + 1, 7)
    return below, above, jnp.where((i == 0) | (i == 7), 1.0, 0.5)


def gradients(cur, i):
    below, above, scale = i_span(i)
    grads = []
    for r in range(3):
        s = slab(cur, r, i)
        row = [
            (slab(cur, r, above) - slab(cur, r, below)) * (UNIT_LENGTH * scale),
            along_j(s) * UNIT_LENGTH,
            along_k(s) * UNIT_LENGTH,
        ]
        row[r] = row[r] + 1.0
        grads.append(row)
    return grads


def cofactors(f):
    return [
        [
            f[1][1] * f[2][2] - f[1][2] * f[2][1],
            f[1][2] * f[2][0] - f[1][0] * f[2][2],
            f[1][0] * f[2][1] - f[1][1] * f[2][0],
        ],
        [
            f[0][2] * f[2][1] - f[0][1] * f[2][2],
            f[0][0] * f[2][2] - f[0][2] * f[2][0],
            f[0][1] * f[2][0] - f[0][0] * f[2][1],
        ],
        [
            f[0][1] * f[1][2] - f[0][2] * f[1][1],
            f[0][2] * f[1][0] - f[0][0] * f[1][2],
            f[0][0] * f[1][1] - f[0][1] * f[1][0],
        ],
    ]


def kernel(
    n_grp,
    n_blk,
    state_ref,
    material_ref,
    occupied_ref,
    column_ref,
    octant_ref,
    out_ref,
    cur,
    mat,
    perm,
    oct_send,
    dil_send,
    dil_rows,
    press_in,
    press,
    face_in,
    fill_in,
    fill_send,
    piola,
    part,
    oct_in,
    dil_in,
    press_send,
    hits,
    select,
    pieces,
    phi_a,
    phi_b,
    diff,
    pi_rows,
    load_sem,
    oct_send_sem,
    oct_sem,
    dil_send_sem,
    dil_sem,
    press_send_sem,
    press_sem,
    face_send_sem,
    face_sem,
    fill_send_sem,
    fill_sem,
    halo_send_sem,
    halo_sem,
    rim_send_sem,
    rim_sem,
):
    grp, blk = lax.axis_index("grp"), lax.axis_index("blk")
    n_mech = n_grp - 1
    solvent = grp == n_mech
    barrier = pltpu.get_barrier_semaphore()
    has_below, has_above = blk > 0, blk < n_blk - 1
    loads = [
        pltpu.make_async_copy(state_ref, cur, load_sem.at[0]),
        pltpu.make_async_copy(material_ref, mat, load_sem.at[1]),
    ]
    for copy in loads:
        copy.start()

    def greet(g, c):
        pl.semaphore_signal(barrier, inc=1, device_id=(g, c), device_id_type=MESH)

    @pl.when(has_below)
    def _():
        greet(grp, blk - 1)

    @pl.when(has_above)
    def _():
        greet(grp, blk + 1)

    beside = jnp.where(has_below, 1, 0) + jnp.where(has_above, 1, 0)

    def send(src, dst, send_sem, recv_sem, g, c):
        copy = pltpu.make_async_remote_copy(
            src_ref=src,
            dst_ref=dst,
            send_sem=send_sem,
            recv_sem=recv_sem,
            device_id=(g, c),
            device_id_type=MESH,
        )
        copy.start()

    def mechanics():
        def greet_column(it, carry):
            greet(n_mech, lax.rem(blk + it, n_blk))
            return carry

        lax.fori_loop(0, n_blk, greet_column, 0)
        filled = occupied_ref[...].astype(F32)
        column = column_ref[...].astype(F32)
        square = (LANES, LANES)
        across = jnp.broadcast_to(column, square)
        diagonal = iota(square, 0) == iota(square, 1)
        down = jnp.sum(jnp.where(diagonal, across, 0.0), axis=1, keepdims=True)
        before = (down == across) & (iota(square, 0) < iota(square, 1))
        rank = jnp.sum(flag(before), axis=0, keepdims=True)
        slot = column * CAP + rank
        slots = n_blk * CAP
        hit = iota((slots, LANES), 0).astype(F32) == slot
        perm[...] = flag(hit, BF16)
        wanted = jnp.sum(
            jnp.where(hit, octant_ref[...].astype(F32) + 1.0, 0.0), axis=1, keepdims=True
        )
        oct_send[...] = jnp.broadcast_to(wanted - 1.0, (slots, LANES)).reshape(n_blk, CAP, LANES)
        fill_send[...] = jnp.broadcast_to(filled, (8, LANES))
        k = iota((8, LANES), 0)
        e = iota((8, LANES), 1)
        filled_8 = jnp.broadcast_to(filled, (8, LANES))
        fill_below = jnp.where(e == 0, 0.0, pltpu.roll(filled_8, 1, 1))
        fill_above = jnp.where(e == LANES - 1, 0.0, pltpu.roll(filled_8, LANES - 1, 1))
        k_weight = (PENALTY * UNIT_LENGTH) * jnp.where(
            k == 0, fill_below, jnp.where(k == 7, fill_above, 0.0)
        )

        pl.semaphore_wait(barrier, n_blk + beside)

        mine = grp * n_blk + blk

        def send_octants(it, carry):
            c = lax.rem(blk + 11 * grp + it, n_blk)
            send(oct_send.at[c], oct_in.at[mine], oct_send_sem, oct_sem, n_mech, c)
            return carry

        lax.fori_loop(0, n_blk, send_octants, 0)

        @pl.when(has_above)
        def _():
            send(fill_send, fill_in.at[0], fill_send_sem.at[1], fill_sem.at[0], grp, blk + 1)

        @pl.when(has_below)
        def _():
            send(fill_send, fill_in.at[1], fill_send_sem.at[0], fill_sem.at[1], grp, blk - 1)

        @pl.when(jnp.logical_not(has_below))
        def _():
            fill_in[0] = jnp.zeros((8, LANES), F32)
            for step in range(STEPS):
                face_in[step, 0] = jnp.zeros((192, LANES), F32)

        @pl.when(jnp.logical_not(has_above))
        def _():
            fill_in[1] = jnp.zeros((8, LANES), F32)
            for step in range(STEPS):
                face_in[step, 1] = jnp.zeros((192, LANES), F32)

        loads[0].wait()

        def dilate(i, carry):
            f = gradients(cur, i)
            det = (
                f[0][0] * (f[1][1] * f[2][2] - f[1][2] * f[2][1])
                - f[0][1] * (f[1][0] * f[2][2] - f[1][2] * f[2][0])
                + f[0][2] * (f[1][0] * f[2][1] - f[1][1] * f[2][0])
            )
            change = (det - 1.0) * filled * DILATION_SCALE
            row = pl.multiple_of(i * 64, 64)
            dil_rows[pl.ds(row, 64), :] = change.reshape(64, LANES).astype(BF16)
            return carry

        def elastic(i, carry):
            f = gradients(cur, i)
            shear, lame = slab(mat, 0, i), slab(mat, 1, i)
            c = [[None] * 3 for _ in range(3)]
            for a in range(3):
                for b in range(a, 3):
                    c[a][b] = f[0][a] * f[0][b] + f[1][a] * f[1][b] + f[2][a] * f[2][b]
                c[a][a] = c[a][a] - 1.0
            trace = (0.5 * lame) * (c[0][0] + c[1][1] + c[2][2])
            s = [[None] * 3 for _ in range(3)]
            for a in range(3):
                for b in range(a, 3):
                    s[a][b] = s[b][a] = shear * c[a][b]
            for a in range(3):
                s[a][a] = s[a][a] + trace
            for r in range(3):
                p = [f[r][0] * s[0][j] + f[r][1] * s[1][j] + f[r][2] * s[2][j] for j in range(3)]
                put_slab(piola, r, i, p[0])
                put_slab(part, r, i, along_j(p[1]) + along_k(p[2]))
            return carry

        def swell(i, carry):
            cof = cofactors(gradients(cur, i))
            row = pl.multiple_of(i * 64, 64)
            pressure = press[pl.ds(row, 64), :].reshape(8, 8, LANES)
            for r in range(3):
                p = [pressure * cof[r][j] for j in range(3)]
                put_slab(piola, r, i, slab(piola, r, i) - p[0])
                put_slab(part, r, i, slab(part, r, i) - (along_j(p[1]) + along_k(p[2])))
            return carry

        def advance(i, carry):
            below, above, scale = i_span(i)
            gain = (TIME_STEP / UNIT_LENGTH) * slab(mat, 2, i) * filled
            at_first = iota((8, 8, LANES), 1) == 0
            for r in range(3):
                s = slab(cur, r, i)
                force = slab(part, r, i) + (slab(piola, r, above) - slab(piola, r, below)) * scale
                z_below = pltpu.roll(pltpu.roll(s, 1, 1), 1, 2)
                z_above = pltpu.roll(pltpu.roll(s, 7, 1), LANES - 1, 2)
                force = force + k_weight * (jnp.where(at_first, z_below, z_above) - s)
                put_slab(cur, r, i, s + gain * force)
            return carry

        for step in range(STEPS):
            if step == 0:
                loads_done = None
            for r in range(3):

                @pl.when(has_above)
                def _():
                    send(
                        cur.at[pl.ds(r * 512 + 448, 64)],
                        face_in.at[step, 0, pl.ds(r * 64, 64)],
                        face_send_sem.at[step, 1],
                        face_sem.at[step, 0],
                        grp,
                        blk + 1,
                    )

                @pl.when(has_below)
                def _():
                    send(
                        cur.at[pl.ds(r * 512, 64)],
                        face_in.at[step, 1, pl.ds(r * 64, 64)],
                        face_send_sem.at[step, 0],
                        face_sem.at[step, 1],
                        grp,
                        blk - 1,
                    )

            lax.fori_loop(0, 8, dilate, 0)
            if step > 0:
                wait_all(dil_send, dil_send_sem.at[step - 1])
            taken = lax.dot_general(
                perm[...], dil_rows[...], (((1,), (1,)), ((), ())), preferred_element_type=F32
            )
            dil_send[...] = taken.reshape(n_blk, CAP, NODES).astype(BF16)

            def send_dilation(it, carry):
                c = lax.rem(blk + 11 * grp + it, n_blk)
                send(
                    dil_send.at[c],
                    dil_in.at[step, mine],
                    dil_send_sem.at[step],
                    dil_sem.at[step],
                    n_mech,
                    c,
                )
                return carry

            lax.fori_loop(0, n_blk, send_dilation, 0)
            if step == 0:
                loads[1].wait()
            lax.fori_loop(0, 8, elastic, 0)
            wait_all(press_in.at[step], press_sem.at[step])
            arrived = press_in[step].astype(F32).reshape(slots, NODES).astype(BF16)
            press[...] = PRESSURE_SCALE * lax.dot_general(
                arrived, perm[...], (((0,), (0,)), ((), ())), preferred_element_type=F32
            )
            lax.fori_loop(0, 8, swell, 0)
            for side, present in ((0, has_below), (1, has_above)):

                @pl.when(present)
                def _():
                    wait_all(face_in.at[step, side], face_sem.at[step, side])
                    wait_all(face_in.at[step, side], face_send_sem.at[step, side])
                    if step == 0:
                        wait_all(fill_send, fill_sem.at[side])
                        wait_all(fill_send, fill_send_sem.at[side])

                at = 7 * side
                weight = (PENALTY * UNIT_LENGTH) * fill_in[side]
                for r in range(3):
                    other = face_in[step, side, pl.ds(r * 64, 64), :].reshape(8, 8, LANES)
                    extra = weight * (other - slab(cur, r, at))
                    put_slab(part, r, at, slab(part, r, at) + extra)
            lax.fori_loop(0, 8, advance, 0)
        wait_all(oct_send, oct_send_sem)
        wait_all(dil_send, dil_send_sem.at[STEPS - 1])

    def brick():
        def greet_elements(it, carry):
            m = lax.rem(3 * blk + it, n_mech * n_blk)
            greet(m // n_blk, lax.rem(m, n_blk))
            return carry

        lax.fori_loop(0, n_mech * n_blk, greet_elements, 0)
        row = iota((768, LANES), 0)
        at_octant = row // 8 == iota((768, LANES), 1)
        for k in range(8):
            select[:, k * LANES : (k + 1) * LANES] = flag(at_octant & (row % 8 == k), BF16)
        q = iota((8, LANES), 1)
        k_at = iota((8, LANES), 0)
        inside = flag((k_at < 7) | (q < DEPTH_OCTANTS - 1))

        def split(value, row, lanes):
            high = value.astype(BF16)
            rest = value - high.astype(F32)
            middle = rest.astype(BF16)
            low = (rest - middle.astype(F32)).astype(BF16)
            for at, piece in enumerate((high, middle, low)):
                pieces[at * 256 + row : at * 256 + row + 256, lanes] = piece

        def joined(product):
            return product[0:256] + product[256:512] + product[512:768]

        def to_layers(source, target, first_row, scale):
            for zq in range(6):
                split(source[pl.ds(zq, 256, stride=6), :], 0, slice(zq * LANES, zq * LANES + LANES))
            for pair in range(4):
                lanes = slice(pair * 256, pair * 256 + 256)
                both = joined(
                    jnp.dot(pieces[:, 0:768], select[:, lanes], preferred_element_type=F32)
                )
                for half in range(2):
                    target[pl.ds(first_row + 2 * pair + half, 256, stride=8), :] = (
                        scale * both[:, half * LANES : (half + 1) * LANES]
                    )

        def from_layers(source, first_row, target):
            for k in range(8):
                lanes = slice(k * LANES, (k + 1) * LANES)
                split(source[pl.ds(first_row + k, 256, stride=8), :], 0, lanes)
            for pair in range(3):
                both = joined(
                    lax.dot_general(
                        pieces[...],
                        select[pair * 256 : pair * 256 + 256, :],
                        (((1,), (1,)), ((), ())),
                        preferred_element_type=F32,
                    )
                )
                for half in range(2):
                    target[pl.ds(2 * pair + half, 256, stride=6), :] = both[
                        :, half * LANES : (half + 1) * LANES
                    ]

        def layer(ref, at):
            return rows_of(ref, at * LAYER, LAYER).reshape(16, 8, LANES)

        def half_weight(v):
            return 0.25 + 0.5 * v * v

        def sweep(source, source_first, target, target_first, diff_first, count):
            start = layer(source, source_first)
            before = layer(source, source_first - 1)
            flux = (half_weight(start) + half_weight(before)) * (start - before)
            in_k = iota((16, 8, LANES), 1)

            def one_layer(x, carry):
                centre, entering = carry
                ahead = layer(source, source_first + 1 + x)
                weight = half_weight(centre)
                leaving = (weight + half_weight(ahead)) * (ahead - centre)
                inflow = leaving - entering
                along_y = (weight[1:] + weight[:-1]) * (centre[1:] - centre[:-1])
                none = jnp.zeros((1, 8, LANES), F32)
                inflow = inflow + (
                    jnp.concatenate([along_y, none], axis=0)
                    - jnp.concatenate([none, along_y], axis=0)
                )
                shifted = pltpu.roll(centre, 7, 1)
                upper = jnp.where(in_k == 7, pltpu.roll(shifted, LANES - 1, 2), shifted)
                along_z = inside * ((weight + half_weight(upper)) * (upper - centre))
                shifted = pltpu.roll(along_z, 1, 1)
                inflow = inflow + (
                    along_z - jnp.where(in_k == 0, pltpu.roll(shifted, 1, 2), shifted)
                )
                updated = centre + layer(diff, diff_first + x) * inflow
                at = pl.multiple_of((target_first + x) * LAYER, LAYER)
                target[pl.ds(at, LAYER), :] = updated.reshape(LAYER, LANES)
                return ahead, leaving

            lax.fori_loop(0, count, one_layer, (start, flux))

        loads[0].wait()
        to_layers(cur, phi_a.at[0], 2 * LAYER, 1.0)

        def octant_block(ref, t, first):
            x, y = 8 * (t // 2), 8 * (t % 2)
            return [rows_of(ref, ((first + x + i) * 16 + y) * 8, 64) for i in range(8)]

        def make_pressure(step):
            for t in range(4):
                value = jnp.concatenate(octant_block(phi_a.at[step], t, 2), axis=0)
                value = value + CUBIC_TERM * value * value * value
                pi_rows[:, t * LANES : (t + 1) * LANES] = value.astype(BF16)

        def send_pressure(step):
            for g in range(n_mech):
                rows = slice(g * n_blk * CAP, (g + 1) * n_blk * CAP)
                taken = lax.dot_general(
                    hits[rows, :],
                    pi_rows[...],
                    (((1,), (1,)), ((), ())),
                    preferred_element_type=F32,
                )
                press_send[step, g * n_blk : (g + 1) * n_blk] = taken.reshape(
                    n_blk, CAP, NODES
                ).astype(BF16)

                def send_one(it, carry):
                    c = lax.rem(blk + 11 * g + it, n_blk)
                    send(
                        press_send.at[step, g * n_blk + c],
                        press_in.at[step, blk],
                        press_send_sem.at[step],
                        press_sem.at[step],
                        g,
                        c,
                    )
                    return carry

                lax.fori_loop(0, n_blk, send_one, 0)

        make_pressure(0)
        pl.semaphore_wait(barrier, n_mech * n_blk + beside)
        wait_all(oct_in, oct_sem)
        wanted = oct_in[...].reshape(n_mech * n_blk * CAP, LANES)
        lane = iota(wanted.shape, 1)
        for t in range(4):
            mine = (wanted == (lane + t * DEPTH_OCTANTS).astype(F32)) & (lane < DEPTH_OCTANTS)
            hits[:, t * LANES : (t + 1) * LANES] = flag(mine, BF16)
        send_pressure(0)
        loads[1].wait()
        to_layers(mat, diff, LAYER, SWEEP_STEP)

        @pl.when(has_above)
        def _():
            send(
                diff.at[pl.ds(16 * LAYER, LAYER)],
                diff.at[pl.ds(0, LAYER)],
                rim_send_sem.at[1],
                rim_sem.at[0],
                grp,
                blk + 1,
            )

        @pl.when(has_below)
        def _():
            send(
                diff.at[pl.ds(LAYER, LAYER)],
                diff.at[pl.ds(17 * LAYER, LAYER)],
                rim_send_sem.at[0],
                rim_sem.at[1],
                grp,
                blk - 1,
            )

        @pl.when(jnp.logical_not(has_below))
        def _():
            diff[0:LAYER, :] = jnp.zeros((LAYER, LANES), F32)
            for step in range(STEPS):
                phi_a[step, 0 : 2 * LAYER, :] = jnp.zeros((2 * LAYER, LANES), F32)

        @pl.when(jnp.logical_not(has_above))
        def _():
            diff[17 * LAYER : 18 * LAYER, :] = jnp.zeros((LAYER, LANES), F32)
            for step in range(STEPS):
                phi_a[step, 18 * LAYER : 20 * LAYER, :] = jnp.zeros((2 * LAYER, LANES), F32)

        for step in range(STEPS):
            phi = phi_a.at[step]
            if step > 0:
                make_pressure(step)
                send_pressure(step)
            wait_all(dil_in.at[step], dil_sem.at[step])
            arrived = dil_in[step].astype(F32).reshape(n_mech * n_blk * CAP, NODES).astype(BF16)
            for pair in range(2):
                lanes = slice(pair * 256, pair * 256 + 256)
                total = lax.dot_general(
                    arrived, hits[:, lanes], (((0,), (0,)), ((), ())), preferred_element_type=F32
                )
                for half in range(2):
                    x, y = 8 * pair, 8 * half
                    for i in range(8):
                        at = ((2 + x + i) * 16 + y) * 8
                        phi[at : at + 64, :] = phi[at : at + 64, :] + (
                            SWEEP_STEP * SOURCE_RATE
                        ) * total[i * 64 : i * 64 + 64, half * LANES : (half + 1) * LANES]

            @pl.when(has_above)
            def _():
                send(
                    phi.at[pl.ds(16 * LAYER, 2 * LAYER)],
                    phi.at[pl.ds(0, 2 * LAYER)],
                    halo_send_sem.at[step, 1],
                    halo_sem.at[step, 0],
                    grp,
                    blk + 1,
                )

            @pl.when(has_below)
            def _():
                send(
                    phi.at[pl.ds(2 * LAYER, 2 * LAYER)],
                    phi.at[pl.ds(18 * LAYER, 2 * LAYER)],
                    halo_send_sem.at[step, 0],
                    halo_sem.at[step, 1],
                    grp,
                    blk - 1,
                )

            for side, present, first in ((0, has_below, 0), (1, has_above, 18)):

                @pl.when(present)
                def _():
                    two = phi.at[pl.ds(first * LAYER, 2 * LAYER)]
                    wait_all(two, halo_sem.at[step, side])
                    wait_all(two, halo_send_sem.at[step, side])
                    if step == 0:
                        one = diff.at[pl.ds(0, LAYER)]
                        wait_all(one, rim_sem.at[side])
                        wait_all(one, rim_send_sem.at[side])

            sweep(phi, 1, phi_b, 0, 0, 18)
            sweep(phi_b, 1, phi_a.at[(step + 1) % 2], 2, 1, 16)
            wait_all(press_send.at[step], press_send_sem.at[step])
        from_layers(phi_a.at[STEPS % 2], 2 * LAYER, cur)

    @pl.when(solvent)
    def _():
        brick()

    @pl.when(jnp.logical_not(solvent))
    def _():
        mechanics()

    store = pltpu.make_async_copy(cur, out_ref, load_sem.at[0])
    store.start()
    store.wait()


def solution(mesh):
    n_grp, n_blk = mesh.shape["grp"], mesh.shape["blk"]
    n_mech = n_grp - 1
    slots = n_blk * CAP
    dma = pltpu.SemaphoreType.DMA
    vmem = pltpu.VMEM
    whole = (1536, LANES)
    call = pl.pallas_call(
        functools.partial(kernel, n_grp, n_blk),
        out_shape=jax.ShapeDtypeStruct(whole, F32),
        in_specs=[pl.BlockSpec(memory_space=pl.ANY)] * 2 + [pl.BlockSpec(memory_space=vmem)] * 3,
        out_specs=pl.BlockSpec(memory_space=pl.ANY),
        scratch_shapes=[
            vmem(whole, F32),
            vmem(whole, F32),
            vmem((slots, LANES), BF16),
            vmem((n_blk, CAP, LANES), F32),
            vmem((n_blk, CAP, NODES), BF16),
            vmem((NODES, LANES), BF16),
            vmem((STEPS, n_blk, CAP, NODES), BF16),
            vmem((NODES, LANES), F32),
            vmem((STEPS, 2, 192, LANES), F32),
            vmem((2, 8, LANES), F32),
            vmem((8, LANES), F32),
            vmem(whole, F32),
            vmem(whole, F32),
            vmem((n_mech * n_blk, CAP, LANES), F32),
            vmem((STEPS, n_mech * n_blk, CAP, NODES), BF16),
            vmem((STEPS, n_mech * n_blk, CAP, NODES), BF16),
            vmem((n_mech * n_blk * CAP, NODES), BF16),
            vmem((768, 1024), BF16),
            vmem((768, 1024), BF16),
            vmem((2, 20 * LAYER, LANES), F32),
            vmem((18 * LAYER, LANES), F32),
            vmem((18 * LAYER, LANES), F32),
            vmem((NODES, NODES), BF16),
            dma((2,)),
            dma,
            dma,
            dma((STEPS,)),
            dma((STEPS,)),
            dma((STEPS,)),
            dma((STEPS,)),
            dma((STEPS, 2)),
            dma((STEPS, 2)),
            dma((2,)),
            dma((2,)),
            dma((STEPS, 2)),
            dma((STEPS, 2)),
            dma((2,)),
            dma((2,)),
        ],
        compiler_params=pltpu.CompilerParams(
            collective_id=0, has_side_effects=True, vmem_limit_bytes=48 << 20
        ),
    )

    def shards(state, material, occupied, brick_column, brick_octant):
        out = call(
            state.reshape(whole),
            material.reshape(whole),
            occupied.reshape(1, LANES),
            brick_column.reshape(1, LANES),
            brick_octant.reshape(1, LANES),
        )
        return out.reshape(state.shape)

    in_specs = (
        P("grp", None, None, "blk"),
        P("grp", None, None, "blk"),
        P(("grp", "blk")),
        P(("grp", "blk"), None),
        P(("grp", "blk")),
    )
    out_specs = P("grp", None, None, "blk")
    return jax.shard_map(shards, mesh=mesh, in_specs=in_specs, out_specs=out_specs, check_vma=False)
```

profile of v0, /device:TPU:23, one launch (start us, length us, event | category | flops | bytes accessed | tf_op | source)
XLA Modules:
  0.0 59.2 jit_solution(1719256715559864573)
XLA Ops:
  0.0 0.0 copy-start.2
  0.0 0.0 copy-start.3
  0.0 0.0 copy-start.4
  0.0 0.6 %copy-done.2 = s32[128]{0:T(128)S(1)} copy-done((s32[128]{0:T(128)S(1)}, s32[128]{0:T(128)}, u32[]{:S(2)}) %copy-start.2) | copy-done | bytes 536
  0.7 0.0 copy-done.3
  0.7 0.0 copy-done.4
  0.7 0.0 copy-start
  0.7 1.1 %copy-done = f32[1,3,512,128]{3,2,1,0:T(8,128)S(1)} copy-done((f32[1,3,512,128]{3,2,1,0:T(8,128)S(1)}, f32[1,3,512,128]{3,2,1,0:T(8,128)}, u32[]{:S(2)}) %copy-start) | copy-done | bytes 786456
  1.8 0.0 copy-start.1
  1.8 1.1 %copy-done.1 = f32[1,3,512,128]{3,2,1,0:T(8,128)S(1)} copy-done((f32[1,3,512,128]{3,2,1,0:T(8,128)S(1)}, f32[1,3,512,128]{3,2,1,0:T(8,128)}, u32[]{:S(2)}) %copy-start.1) | copy-done | bytes 786456
  3.0 55.4 %shard_map.55 = f32[1536,128]{1,0:T(8,128)S(1)} custom-call(f32[1536,128]{1,0:T(8,128)S(1)} %bitcast.7, f32[1536,128]{1,0:T(8,128)S(1)} %bitcast.8, s32[1,128]{1,0:T(1,128)S(1)} %bitcast.9, s32[1,128]{1,0:T(1,128)S(1)} %bitcast.10, s32[1,128]{1,0:T(1,128)S(1)} %bitcast.11), custom_call_target="tpu_custom_call" | custom-call | tf_op jit(solution)/shard_map/pallas_call | solution.py:699
  58.3 0.9 %copy.7 = f32[1,3,512,128]{3,2,1,0:T(8,128)} copy(f32[1,3,512,128]{3,2,1,0:T(8,128)S(1)} %bitcast.6) | data formatting | bytes 1572864
Async XLA Ops:
  0.0 0.7 %copy-start.2 = (s32[128]{0:T(128)S(1)}, s32[128]{0:T(128)}, u32[]{:S(2)}) copy-start(s32[128]{0:T(128)} %param.7) | copy-start | bytes 1540
  0.0 0.7 %copy-start.3 = (s32[128,1]{0,1:T(1,128)S(1)}, s32[128,1]{0,1:T(1,128)}, u32[]{:S(2)}) copy-start(s32[128,1]{0,1:T(1,128)} %param.8) | copy-start | bytes 1540
  0.0 0.7 %copy-start.4 = (s32[128]{0:T(128)S(1)}, s32[128]{0:T(128)}, u32[]{:S(2)}) copy-start(s32[128]{0:T(128)} %param.9) | copy-start | bytes 1540
  0.7 1.1 %copy-start = (f32[1,3,512,128]{3,2,1,0:T(8,128)S(1)}, f32[1,3,512,128]{3,2,1,0:T(8,128)}, u32[]{:S(2)}) copy-start(f32[1,3,512,128]{3,2,1,0:T(8,128)} %param.5) | copy-start | bytes 2359300
  1.8 1.1 %copy-start.1 = (f32[1,3,512,128]{3,2,1,0:T(8,128)S(1)}, f32[1,3,512,128]{3,2,1,0:T(8,128)}, u32[]{:S(2)}) copy-start(f32[1,3,512,128]{3,2,1,0:T(8,128)} %param.6) | copy-start | bytes 2359300
where the time goes:
time: 59.4 us; the launch traced here: 59.2 us
  Pallas kernels  55.4 us (93%)
  local copies, waits for them, and re-layouts  3.83 us (6%)
    pallas_call x1, Pallas kernels, shards(): call(state.reshape(whole), material.reshape(whole), occupied.reshape(1, L...  55.4 us
    unnamed x11, local copies, waits for them, and re-layouts  3.83 us

commit v1 on v0

--- a/solution.py
+++ b/solution.py
@@ -1,3 +1,4 @@
+import contextlib
 import functools
 
 import jax
@@ -24,7 +25,13 @@
 NODES = 512
 CAP = 8
 DEPTH_OCTANTS = 96
+CODE_SHIFT = 191.0
+EMPTY_CODE = -1000.0
 LAYER = 128
+
+
+def phase(name):
+    return contextlib.nullcontext()
 
 
 def iota(shape, dim):
@@ -111,9 +118,11 @@
     occupied_ref,
     column_ref,
     octant_ref,
-    out_ref,
     cur,
     mat,
+    occupied_in,
+    column_in,
+    octant_in,
     perm,
     oct_send,
     dil_send,
@@ -125,6 +134,7 @@
     fill_send,
     piola,
     part,
+    cofactor,
     oct_in,
     dil_in,
     press_send,
@@ -135,7 +145,9 @@
     phi_b,
     diff,
     pi_rows,
+    total,
     load_sem,
+    small_sem,
     oct_send_sem,
     oct_sem,
     dil_send_sem,
@@ -188,27 +200,46 @@
         copy.start()
 
     def mechanics():
-        def greet_column(it, carry):
-            greet(n_mech, lax.rem(blk + it, n_blk))
-            return carry
-
-        lax.fori_loop(0, n_blk, greet_column, 0)
-        filled = occupied_ref[...].astype(F32)
-        column = column_ref[...].astype(F32)
+        small = [
+            pltpu.make_async_copy(source, target, small_sem.at[at])
+            for at, (source, target) in enumerate(
+                (
+                    (occupied_ref, occupied_in),
+                    (column_ref, column_in),
+                    (octant_ref, octant_in),
+                )
+            )
+        ]
+        for copy in small:
+            copy.start()
+        with phase("m_small"):
+            for copy in small:
+                copy.wait()
+        filled = occupied_in[...].astype(F32)
+        column = column_in[...].astype(F32)
+        octant = octant_in[...].astype(F32)
         square = (LANES, LANES)
         across = jnp.broadcast_to(column, square)
         diagonal = iota(square, 0) == iota(square, 1)
         down = jnp.sum(jnp.where(diagonal, across, 0.0), axis=1, keepdims=True)
-        before = (down == across) & (iota(square, 0) < iota(square, 1))
-        rank = jnp.sum(flag(before), axis=0, keepdims=True)
+        same = down == across
+        rank = jnp.sum(flag(same & (iota(square, 0) < iota(square, 1))), axis=0, keepdims=True)
+        rank_down = jnp.sum(
+            flag(same & (iota(square, 1) < iota(square, 0))), axis=1, keepdims=True
+        )
         slot = column * CAP + rank
         slots = n_blk * CAP
         hit = iota((slots, LANES), 0).astype(F32) == slot
         perm[...] = flag(hit, BF16)
-        wanted = jnp.sum(
-            jnp.where(hit, octant_ref[...].astype(F32) + 1.0, 0.0), axis=1, keepdims=True
-        )
-        oct_send[...] = jnp.broadcast_to(wanted - 1.0, (slots, LANES)).reshape(n_blk, CAP, LANES)
+        at_column = iota((n_blk, LANES), 0).astype(F32) == column
+        coded = jnp.concatenate(
+            [jnp.where(at_column, octant - CODE_SHIFT, 0.0), flag(at_column)], axis=0
+        ).astype(BF16)
+        at_rank = flag(iota(square, 1).astype(F32) == rank_down, BF16)
+        placed = jnp.dot(coded, at_rank, preferred_element_type=F32)
+        code = placed[0:n_blk] + EMPTY_CODE * (1.0 - placed[n_blk : 2 * n_blk])
+        for c in range(n_blk):
+            oct_send[c] = code[c : c + 1, :]
         fill_send[...] = jnp.broadcast_to(filled, (8, LANES))
         k = iota((8, LANES), 0)
         e = iota((8, LANES), 1)
@@ -219,7 +250,8 @@
             k == 0, fill_below, jnp.where(k == 7, fill_above, 0.0)
         )
 
-        pl.semaphore_wait(barrier, n_blk + beside)
+        with phase("m_barrier"):
+            pl.semaphore_wait(barrier, n_blk + beside)
 
         mine = grp * n_blk + blk
 
@@ -228,15 +260,8 @@
             send(oct_send.at[c], oct_in.at[mine], oct_send_sem, oct_sem, n_mech, c)
             return carry
 
-        lax.fori_loop(0, n_blk, send_octants, 0)
-
-        @pl.when(has_above)
-        def _():
-            send(fill_send, fill_in.at[0], fill_send_sem.at[1], fill_sem.at[0], grp, blk + 1)
-
-        @pl.when(has_below)
-        def _():
-            send(fill_send, fill_in.at[1], fill_send_sem.at[0], fill_sem.at[1], grp, blk - 1)
+        with phase("m_send_oct"):
+            lax.fori_loop(0, n_blk, send_octants, 0)
 
         @pl.when(jnp.logical_not(has_below))
         def _():
@@ -250,7 +275,8 @@
             for step in range(STEPS):
                 face_in[step, 1] = jnp.zeros((192, LANES), F32)
 
-        loads[0].wait()
+        with phase("m_load"):
+            loads[0].wait()
 
         def dilate(i, carry):
             f = gradients(cur, i)
@@ -260,8 +286,8 @@
                 + f[0][2] * (f[1][0] * f[2][1] - f[1][1] * f[2][0])
             )
             change = (det - 1.0) * filled * DILATION_SCALE
-            row = pl.multiple_of(i * 64, 64)
-            dil_rows[pl.ds(row, 64), :] = change.reshape(64, LANES).astype(BF16)
+            for j in range(8):
+                dil_rows[pl.ds(i * 8 + j, 8, stride=64), :] = change[j]
             return carry
 
         def elastic(i, carry):
@@ -283,14 +309,18 @@
                 p = [f[r][0] * s[0][j] + f[r][1] * s[1][j] + f[r][2] * s[2][j] for j in range(3)]
                 put_slab(piola, r, i, p[0])
                 put_slab(part, r, i, along_j(p[1]) + along_k(p[2]))
+            cof = cofactors(f)
+            for r in range(3):
+                for j in range(3):
+                    put_slab(cofactor, 3 * r + j, i, cof[r][j])
             return carry
 
         def swell(i, carry):
-            cof = cofactors(gradients(cur, i))
-            row = pl.multiple_of(i * 64, 64)
-            pressure = press[pl.ds(row, 64), :].reshape(8, 8, LANES)
+            pressure = jnp.concatenate(
+                [press[pl.ds(i * 8 + j, 8, stride=64), :][None] for j in range(8)], axis=0
+            )
             for r in range(3):
-                p = [pressure * cof[r][j] for j in range(3)]
+                p = [pressure * slab(cofactor, 3 * r + j, i) for j in range(3)]
                 put_slab(piola, r, i, slab(piola, r, i) - p[0])
                 put_slab(part, r, i, slab(part, r, i) - (along_j(p[1]) + along_k(p[2])))
             return carry
@@ -309,8 +339,57 @@
             return carry
 
         for step in range(STEPS):
+            with phase("m_dilate"):
+                lax.fori_loop(0, 8, dilate, 0)
+            if step > 0:
+                wait_all(dil_send, dil_send_sem.at[step - 1])
+            with phase("m_take"):
+                taken = lax.dot_general(
+                    perm[...],
+                    dil_rows[...].astype(BF16),
+                    (((1,), (1,)), ((), ())),
+                    preferred_element_type=F32,
+                )
+                dil_send[...] = taken.reshape(n_blk, CAP, NODES).astype(BF16)
+
+            def send_dilation(it, carry):
+                c = lax.rem(blk + 11 * grp + it, n_blk)
+                send(
+                    dil_send.at[c],
+                    dil_in.at[step, mine],
+                    dil_send_sem.at[step],
+                    dil_sem.at[step],
+                    n_mech,
+                    c,
+                )
+                return carry
+
+            with phase("m_send_dil"):
+                lax.fori_loop(0, n_blk, send_dilation, 0)
             if step == 0:
-                loads_done = None
+
+                @pl.when(has_above)
+                def _():
+                    send(
+                        fill_send,
+                        fill_in.at[0],
+                        fill_send_sem.at[1],
+                        fill_sem.at[0],
+                        grp,
+                        blk + 1,
+                    )
+
+                @pl.when(has_below)
+                def _():
+                    send(
+                        fill_send,
+                        fill_in.at[1],
+                        fill_send_sem.at[0],
+                        fill_sem.at[1],
+                        grp,
+                        blk - 1,
+                    )
+
             for r in range(3):
 
                 @pl.when(has_above)
@@ -334,37 +413,19 @@
                         grp,
                         blk - 1,
                     )
-
-            lax.fori_loop(0, 8, dilate, 0)
-            if step > 0:
-                wait_all(dil_send, dil_send_sem.at[step - 1])
-            taken = lax.dot_general(
-                perm[...], dil_rows[...], (((1,), (1,)), ((), ())), preferred_element_type=F32
-            )
-            dil_send[...] = taken.reshape(n_blk, CAP, NODES).astype(BF16)
-
-            def send_dilation(it, carry):
-                c = lax.rem(blk + 11 * grp + it, n_blk)
-                send(
-                    dil_send.at[c],
-                    dil_in.at[step, mine],
-                    dil_send_sem.at[step],
-                    dil_sem.at[step],
-                    n_mech,
-                    c,
-                )
-                return carry
-
-            lax.fori_loop(0, n_blk, send_dilation, 0)
             if step == 0:
                 loads[1].wait()
-            lax.fori_loop(0, 8, elastic, 0)
-            wait_all(press_in.at[step], press_sem.at[step])
-            arrived = press_in[step].astype(F32).reshape(slots, NODES).astype(BF16)
-            press[...] = PRESSURE_SCALE * lax.dot_general(
-                arrived, perm[...], (((0,), (0,)), ((), ())), preferred_element_type=F32
-            )
-            lax.fori_loop(0, 8, swell, 0)
+            with phase("m_elastic"):
+                lax.fori_loop(0, 8, elastic, 0)
+            with phase("m_wait_press"):
+                wait_all(press_in.at[step], press_sem.at[step])
+            with phase("m_press"):
+                arrived = press_in[step].astype(F32).reshape(slots, NODES).astype(BF16)
+                press[...] = PRESSURE_SCALE * lax.dot_general(
+                    arrived, perm[...], (((0,), (0,)), ((), ())), preferred_element_type=F32
+                )
+            with phase("m_swell"):
+                lax.fori_loop(0, 8, swell, 0)
             for side, present in ((0, has_below), (1, has_above)):
 
                 @pl.when(present)
@@ -381,117 +442,144 @@
                     other = face_in[step, side, pl.ds(r * 64, 64), :].reshape(8, 8, LANES)
                     extra = weight * (other - slab(cur, r, at))
                     put_slab(part, r, at, slab(part, r, at) + extra)
-            lax.fori_loop(0, 8, advance, 0)
+            with phase("m_advance"):
+                lax.fori_loop(0, 8, advance, 0)
         wait_all(oct_send, oct_send_sem)
         wait_all(dil_send, dil_send_sem.at[STEPS - 1])
 
     def brick():
-        def greet_elements(it, carry):
-            m = lax.rem(3 * blk + it, n_mech * n_blk)
-            greet(m // n_blk, lax.rem(m, n_blk))
-            return carry
-
-        lax.fori_loop(0, n_mech * n_blk, greet_elements, 0)
+        with phase("s_greet"):
+            for g in range(n_mech):
+
+                def greet_element(it, carry):
+                    greet(g, lax.rem(blk + 11 * g + it, n_blk))
+                    return carry
+
+                lax.fori_loop(0, n_blk, greet_element, 0)
         row = iota((768, LANES), 0)
         at_octant = row // 8 == iota((768, LANES), 1)
         for k in range(8):
             select[:, k * LANES : (k + 1) * LANES] = flag(at_octant & (row % 8 == k), BF16)
-        q = iota((8, LANES), 1)
-        k_at = iota((8, LANES), 0)
-        inside = flag((k_at < 7) | (q < DEPTH_OCTANTS - 1))
-
-        def split(value, row, lanes):
+        def split(value, lanes):
+            count = value.shape[0]
             high = value.astype(BF16)
             rest = value - high.astype(F32)
             middle = rest.astype(BF16)
             low = (rest - middle.astype(F32)).astype(BF16)
             for at, piece in enumerate((high, middle, low)):
-                pieces[at * 256 + row : at * 256 + row + 256, lanes] = piece
+                pieces[at * count : (at + 1) * count, lanes] = piece
 
         def joined(product):
-            return product[0:256] + product[256:512] + product[512:768]
-
-        def to_layers(source, target, first_row, scale):
+            count = product.shape[0] // 3
+            return product[0:count] + product[count : 2 * count] + product[2 * count : 3 * count]
+
+        def to_layers(source, target, first, scale):
             for zq in range(6):
-                split(source[pl.ds(zq, 256, stride=6), :], 0, slice(zq * LANES, zq * LANES + LANES))
+                split(source[pl.ds(zq, 256, stride=6), :], slice(zq * LANES, zq * LANES + LANES))
             for pair in range(4):
                 lanes = slice(pair * 256, pair * 256 + 256)
                 both = joined(
                     jnp.dot(pieces[:, 0:768], select[:, lanes], preferred_element_type=F32)
                 )
                 for half in range(2):
-                    target[pl.ds(first_row + 2 * pair + half, 256, stride=8), :] = (
-                        scale * both[:, half * LANES : (half + 1) * LANES]
-                    )
-
-        def from_layers(source, first_row, target):
+                    value = scale * both[:, half * LANES : (half + 1) * LANES]
+                    for x in range(16):
+                        at = ((first + x) * 8 + 2 * pair + half) * 16
+                        target[at : at + 16, :] = value[x * 16 : x * 16 + 16]
+
+        def from_layers(source, first, spans):
+            count = 16 * sum(last - start for start, last in spans)
             for k in range(8):
-                lanes = slice(k * LANES, (k + 1) * LANES)
-                split(source[pl.ds(first_row + k, 256, stride=8), :], 0, lanes)
+                rows = [
+                    source[at : at + 16, :]
+                    for start, last in spans
+                    for at in [((first + x) * 8 + k) * 16 for x in range(start, last)]
+                ]
+                split(jnp.concatenate(rows, axis=0), slice(k * LANES, (k + 1) * LANES))
             for pair in range(3):
                 both = joined(
                     lax.dot_general(
-                        pieces[...],
+                        pieces[0 : 3 * count, :],
                         select[pair * 256 : pair * 256 + 256, :],
                         (((1,), (1,)), ((), ())),
                         preferred_element_type=F32,
                     )
                 )
                 for half in range(2):
-                    target[pl.ds(2 * pair + half, 256, stride=6), :] = both[
-                        :, half * LANES : (half + 1) * LANES
-                    ]
-
-        def layer(ref, at):
-            return rows_of(ref, at * LAYER, LAYER).reshape(16, 8, LANES)
+                    taken = 0
+                    for start, last in spans:
+                        more = 16 * (last - start)
+                        cur[pl.ds(start * 96 + 2 * pair + half, more, stride=6), :] = both[
+                            taken : taken + more, half * LANES : (half + 1) * LANES
+                        ]
+                        taken += more
 
         def half_weight(v):
             return 0.25 + 0.5 * v * v
 
-        def sweep(source, source_first, target, target_first, diff_first, count):
-            start = layer(source, source_first)
-            before = layer(source, source_first - 1)
-            flux = (half_weight(start) + half_weight(before)) * (start - before)
-            in_k = iota((16, 8, LANES), 1)
+        plane = (1, 16, LANES)
+        not_first = flag(iota(plane, 1) > 0)
+        not_last = flag(iota(plane, 1) < 15)
+        at_start = iota(plane, 2) == 0
+        at_end = iota(plane, 2) >= DEPTH_OCTANTS - 1
+
+        def sweep(source, source_first, target, target_first, diff_first, start, last):
+            source_first, target_first = source_first + start, target_first + start
+            diff_first = diff_first + start
+
+            def rows_from(row):
+                return source[pl.ds(row, LAYER), :].reshape(8, 16, LANES)
 
             def one_layer(x, carry):
-                centre, entering = carry
-                ahead = layer(source, source_first + 1 + x)
+                row = pl.multiple_of((source_first + x) * LAYER, LAYER)
+                centre = rows_from(row)
+                x_below = rows_from(pl.multiple_of(row - LAYER, LAYER))
+                x_above = rows_from(pl.multiple_of(row + LAYER, LAYER))
+                y_below, y_above = rows_from(row - 1), rows_from(row + 1)
                 weight = half_weight(centre)
-                leaving = (weight + half_weight(ahead)) * (ahead - centre)
-                inflow = leaving - entering
-                along_y = (weight[1:] + weight[:-1]) * (centre[1:] - centre[:-1])
-                none = jnp.zeros((1, 8, LANES), F32)
+
+                def flux(there):
+                    return (weight + half_weight(there)) * (there - centre)
+
+                inflow = flux(x_above) + flux(x_below)
+                inflow = inflow + not_last * flux(y_above) + not_first * flux(y_below)
+                after = jnp.where(at_end, centre[7:8], pltpu.roll(centre[0:1], LANES - 1, 2))
+                before = jnp.where(at_start, centre[0:1], pltpu.roll(centre[7:8], 1, 2))
+                inner = (weight[1:] + weight[:-1]) * (centre[1:] - centre[:-1])
+                leave = (weight[7:8] + half_weight(after)) * (after - centre[7:8])
+                enter = (weight[0:1] + half_weight(before)) * (before - centre[0:1])
                 inflow = inflow + (
-                    jnp.concatenate([along_y, none], axis=0)
-                    - jnp.concatenate([none, along_y], axis=0)
-                )
-                shifted = pltpu.roll(centre, 7, 1)
-                upper = jnp.where(in_k == 7, pltpu.roll(shifted, LANES - 1, 2), shifted)
-                along_z = inside * ((weight + half_weight(upper)) * (upper - centre))
-                shifted = pltpu.roll(along_z, 1, 1)
-                inflow = inflow + (
-                    along_z - jnp.where(in_k == 0, pltpu.roll(shifted, 1, 2), shifted)
-                )
-                updated = centre + layer(diff, diff_first + x) * inflow
+                    jnp.concatenate([inner, leave], axis=0)
+                    + jnp.concatenate([enter, -inner], axis=0)
+                )
+                gain = rows_of(diff, (diff_first + x) * LAYER, LAYER).reshape(8, 16, LANES)
+                updated = centre + gain * inflow
                 at = pl.multiple_of((target_first + x) * LAYER, LAYER)
                 target[pl.ds(at, LAYER), :] = updated.reshape(LAYER, LANES)
-                return ahead, leaving
-
-            lax.fori_loop(0, count, one_layer, (start, flux))
-
-        loads[0].wait()
-        to_layers(cur, phi_a.at[0], 2 * LAYER, 1.0)
-
-        def octant_block(ref, t, first):
-            x, y = 8 * (t // 2), 8 * (t % 2)
-            return [rows_of(ref, ((first + x + i) * 16 + y) * 8, 64) for i in range(8)]
+                return carry
+
+            lax.fori_loop(0, last - start, one_layer, 0)
+
+        with phase("s_load"):
+            loads[0].wait()
+        with phase("s_to_layers"):
+            to_layers(cur, phi_a.at[0], 2, 1.0)
 
         def make_pressure(step):
-            for t in range(4):
-                value = jnp.concatenate(octant_block(phi_a.at[step], t, 2), axis=0)
-                value = value + CUBIC_TERM * value * value * value
-                pi_rows[:, t * LANES : (t + 1) * LANES] = value.astype(BF16)
+            phi = phi_a.at[step]
+
+            def one_k(k, carry):
+                for t in range(4):
+                    x, y = 8 * (t // 2), 8 * (t % 2)
+                    value = jnp.concatenate(
+                        [rows_of(phi, ((2 + x + i) * 8 + k) * 16 + y, 8) for i in range(8)], axis=0
+                    )
+                    value = value + CUBIC_TERM * value * value * value
+                    at = pl.multiple_of(k * 64, 64)
+                    pi_rows[pl.ds(at, 64), t * LANES : (t + 1) * LANES] = value.astype(BF16)
+                return carry
+
+            lax.fori_loop(0, 8, one_k, 0)
 
         def send_pressure(step):
             for g in range(n_mech):
@@ -520,17 +608,32 @@
 
                 lax.fori_loop(0, n_blk, send_one, 0)
 
-        make_pressure(0)
-        pl.semaphore_wait(barrier, n_mech * n_blk + beside)
-        wait_all(oct_in, oct_sem)
-        wanted = oct_in[...].reshape(n_mech * n_blk * CAP, LANES)
-        lane = iota(wanted.shape, 1)
-        for t in range(4):
-            mine = (wanted == (lane + t * DEPTH_OCTANTS).astype(F32)) & (lane < DEPTH_OCTANTS)
-            hits[:, t * LANES : (t + 1) * LANES] = flag(mine, BF16)
-        send_pressure(0)
+        with phase("s_pi"):
+            make_pressure(0)
+        with phase("s_barrier"):
+            pl.semaphore_wait(barrier, beside)
+        with phase("s_wait_oct"):
+            wait_all(oct_in, oct_sem)
+        with phase("s_hits"):
+            spread = (n_mech * n_blk, CAP, LANES)
+            one_code = jnp.where(
+                iota(spread, 1) == iota(spread, 2), jnp.broadcast_to(oct_in[...], spread), 0.0
+            )
+            wanted = jnp.dot(
+                one_code.reshape(n_mech * n_blk * CAP, LANES).astype(BF16),
+                jnp.ones((LANES, LANES), BF16),
+                preferred_element_type=F32,
+            )
+            lane = iota(wanted.shape, 1)
+            for t in range(4):
+                at_octant = (lane + t * DEPTH_OCTANTS).astype(F32) - CODE_SHIFT
+                mine = (wanted == at_octant) & (lane < DEPTH_OCTANTS)
+                hits[:, t * LANES : (t + 1) * LANES] = flag(mine, BF16)
+        with phase("s_send_press"):
+            send_pressure(0)
         loads[1].wait()
-        to_layers(mat, diff, LAYER, SWEEP_STEP)
+        with phase("s_to_layers_d"):
+            to_layers(mat, diff, 1, SWEEP_STEP)
 
         @pl.when(has_above)
         def _():
@@ -569,22 +672,33 @@
         for step in range(STEPS):
             phi = phi_a.at[step]
             if step > 0:
-                make_pressure(step)
-                send_pressure(step)
-            wait_all(dil_in.at[step], dil_sem.at[step])
-            arrived = dil_in[step].astype(F32).reshape(n_mech * n_blk * CAP, NODES).astype(BF16)
-            for pair in range(2):
-                lanes = slice(pair * 256, pair * 256 + 256)
-                total = lax.dot_general(
-                    arrived, hits[:, lanes], (((0,), (0,)), ((), ())), preferred_element_type=F32
-                )
-                for half in range(2):
-                    x, y = 8 * pair, 8 * half
-                    for i in range(8):
-                        at = ((2 + x + i) * 16 + y) * 8
-                        phi[at : at + 64, :] = phi[at : at + 64, :] + (
-                            SWEEP_STEP * SOURCE_RATE
-                        ) * total[i * 64 : i * 64 + 64, half * LANES : (half + 1) * LANES]
+                with phase("s_pi"):
+                    make_pressure(step)
+                with phase("s_send_press"):
+                    send_pressure(step)
+            with phase("s_wait_dil"):
+                wait_all(dil_in.at[step], dil_sem.at[step])
+            with phase("s_deposit"):
+                arrived = dil_in[step].astype(F32).reshape(n_mech * n_blk * CAP, NODES).astype(BF16)
+                total[...] = lax.dot_general(
+                    arrived, hits[...], (((0,), (0,)), ((), ())), preferred_element_type=F32
+                )
+
+                def one_k(k, carry):
+                    for t in range(4):
+                        for i in range(8):
+                            x, y = 8 * (t // 2) + i, 8 * (t % 2)
+                            at = pl.multiple_of(((2 + x) * 8 + k) * 16 + y, 8)
+                            more = total[
+                                pl.ds(pl.multiple_of(k * 64 + i * 8, 8), 8),
+                                t * LANES : (t + 1) * LANES,
+                            ]
+                            phi[pl.ds(at, 8), :] = (
+                                phi[pl.ds(at, 8), :] + (SWEEP_STEP * SOURCE_RATE) * more
+                            )
+                    return carry
+
+                lax.fori_loop(0, 8, one_k, 0)
 
             @pl.when(has_above)
             def _():
@@ -608,22 +722,35 @@
                     blk - 1,
                 )
 
-            for side, present, first in ((0, has_below, 0), (1, has_above, 18)):
-
-                @pl.when(present)
-                def _():
-                    two = phi.at[pl.ds(first * LAYER, 2 * LAYER)]
-                    wait_all(two, halo_sem.at[step, side])
-                    wait_all(two, halo_send_sem.at[step, side])
-                    if step == 0:
-                        one = diff.at[pl.ds(0, LAYER)]
-                        wait_all(one, rim_sem.at[side])
-                        wait_all(one, rim_send_sem.at[side])
-
-            sweep(phi, 1, phi_b, 0, 0, 18)
-            sweep(phi_b, 1, phi_a.at[(step + 1) % 2], 2, 1, 16)
-            wait_all(press_send.at[step], press_send_sem.at[step])
-        from_layers(phi_a.at[STEPS % 2], 2 * LAYER, cur)
+            after = phi_a.at[(step + 1) % 2]
+            with phase("s_sweep_inner"):
+                sweep(phi, 2, phi_b, 1, 1, 1, 15)
+                sweep(phi_b, 1, after, 2, 1, 2, 14)
+            if step == STEPS - 1:
+                with phase("s_from_inner"):
+                    from_layers(after, 2, [(2, 14)])
+            with phase("s_wait_halo"):
+                for side, present, first in ((0, has_below, 0), (1, has_above, 18)):
+
+                    @pl.when(present)
+                    def _():
+                        two = phi.at[pl.ds(first * LAYER, 2 * LAYER)]
+                        wait_all(two, halo_sem.at[step, side])
+                        wait_all(two, halo_send_sem.at[step, side])
+                        if step == 0:
+                            one = diff.at[pl.ds(0, LAYER)]
+                            wait_all(one, rim_sem.at[side])
+                            wait_all(one, rim_send_sem.at[side])
+
+            with phase("s_sweep_edge"):
+                sweep(phi, 2, phi_b, 1, 1, -1, 1)
+                sweep(phi, 2, phi_b, 1, 1, 15, 17)
+                sweep(phi_b, 1, after, 2, 1, 0, 2)
+                sweep(phi_b, 1, after, 2, 1, 14, 16)
+            with phase("s_sent"):
+                wait_all(press_send.at[step], press_send_sem.at[step])
+        with phase("s_from_edge"):
+            from_layers(phi_a.at[STEPS % 2], 2, [(0, 2), (14, 16)])
 
     @pl.when(solvent)
     def _():
@@ -632,10 +759,6 @@
     @pl.when(jnp.logical_not(solvent))
     def _():
         mechanics()
-
-    store = pltpu.make_async_copy(cur, out_ref, load_sem.at[0])
-    store.start()
-    store.wait()
 
 
 def solution(mesh):
@@ -648,15 +771,17 @@
     call = pl.pallas_call(
         functools.partial(kernel, n_grp, n_blk),
         out_shape=jax.ShapeDtypeStruct(whole, F32),
-        in_specs=[pl.BlockSpec(memory_space=pl.ANY)] * 2 + [pl.BlockSpec(memory_space=vmem)] * 3,
-        out_specs=pl.BlockSpec(memory_space=pl.ANY),
+        in_specs=[pl.BlockSpec(memory_space=pltpu.HBM)] * 5,
+        out_specs=pl.BlockSpec(memory_space=vmem),
         scratch_shapes=[
             vmem(whole, F32),
-            vmem(whole, F32),
+            vmem((1, LANES), jnp.int32),
+            vmem((1, LANES), jnp.int32),
+            vmem((1, LANES), jnp.int32),
             vmem((slots, LANES), BF16),
-            vmem((n_blk, CAP, LANES), F32),
+            vmem((n_blk, 1, LANES), F32),
             vmem((n_blk, CAP, NODES), BF16),
-            vmem((NODES, LANES), BF16),
+            vmem((NODES, LANES), F32),
             vmem((STEPS, n_blk, CAP, NODES), BF16),
             vmem((NODES, LANES), F32),
             vmem((STEPS, 2, 192, LANES), F32),
@@ -664,7 +789,8 @@
             vmem((8, LANES), F32),
             vmem(whole, F32),
             vmem(whole, F32),
-            vmem((n_mech * n_blk, CAP, LANES), F32),
+            vmem((9 * NODES, LANES), F32),
+            vmem((n_mech * n_blk, 1, LANES), F32),
             vmem((STEPS, n_mech * n_blk, CAP, NODES), BF16),
             vmem((STEPS, n_mech * n_blk, CAP, NODES), BF16),
             vmem((n_mech * n_blk * CAP, NODES), BF16),
@@ -674,7 +800,9 @@
             vmem((18 * LAYER, LANES), F32),
             vmem((18 * LAYER, LANES), F32),
             vmem((NODES, NODES), BF16),
+            vmem((NODES, NODES), F32),
             dma((2,)),
+            dma((3,)),
             dma,
             dma,
             dma((STEPS,)),
@@ -691,7 +819,7 @@
             dma((2,)),
         ],
         compiler_params=pltpu.CompilerParams(
-            collective_id=0, has_side_effects=True, vmem_limit_bytes=48 << 20
+            collective_id=0, has_side_effects=True, vmem_limit_bytes=55 * 1000000
         ),
     )
 

time: 59.4 us -> 43.7 us (0.74)
  the two profiles are of different devices: /device:TPU:23 before, /device:TPU:49 now
where the time goes in v1:
time: 43.7 us; the launch traced here: 43.5 us
  Pallas kernels  42 us (96%)
  local copies, waits for them, and re-layouts  1.56 us (4%)
    pallas_call x1, Pallas kernels, shards(): call(state.reshape(whole), material.reshape(whole), occupied.reshape(1, L...  42 us
    unnamed x7, local copies, waits for them, and re-layouts  1.56 us

profile of v1, /device:TPU:49, one launch (start us, length us, event | category | flops | bytes accessed | tf_op | source)
XLA Modules:
  0.0 43.5 jit_solution(815346082466494245)
XLA Ops:
  0.0 0.0 copy-start
  0.0 0.0 copy-start.1
  0.0 0.0 copy-start.2
  0.0 0.6 %copy-done = s32[128]{0:T(128)S(1)} copy-done((s32[128]{0:T(128)S(1)}, s32[128]{0:T(128)}, u32[]{:S(2)}) %copy-start) | copy-done | bytes 536
  0.7 0.0 copy-done.1
  0.7 0.0 copy-done.2
  0.7 42.0 %shard_map.55 = f32[1536,128]{1,0:T(8,128)S(1)} custom-call(f32[1536,128]{1,0:T(8,128)} %bitcast.10, f32[1536,128]{1,0:T(8,128)} %bitcast.11, s32[1,128]{1,0:T(1,128)S(1)} %bitcast.7, s32[1,128]{1,0:T(1,128)S(1)} %bitcast.8, s32[1,128]{1,0:T(1,128)S(1)} %bitcast.9), custom_call_target="tpu_custom_call" | custom-call | tf_op jit(solution)/shard_map/pallas_call | solution.py:827
  42.7 0.9 %copy.7 = f32[1,3,512,128]{3,2,1,0:T(8,128)} copy(f32[1,3,512,128]{3,2,1,0:T(8,128)S(1)} %bitcast.6) | data formatting | bytes 1572864
Async XLA Ops:
  0.0 0.7 %copy-start = (s32[128]{0:T(128)S(1)}, s32[128]{0:T(128)}, u32[]{:S(2)}) copy-start(s32[128]{0:T(128)} %param.7) | copy-start | bytes 1540
  0.0 0.7 %copy-start.1 = (s32[128,1]{0,1:T(1,128)S(1)}, s32[128,1]{0,1:T(1,128)}, u32[]{:S(2)}) copy-start(s32[128,1]{0,1:T(1,128)} %param.8) | copy-start | bytes 1540
  0.0 0.7 %copy-start.2 = (s32[128]{0:T(128)S(1)}, s32[128]{0:T(128)}, u32[]{:S(2)}) copy-start(s32[128]{0:T(128)} %param.9) | copy-start | bytes 1540

commit v2 on v1

--- a/solution.py
+++ b/solution.py
@@ -27,7 +27,15 @@
 DEPTH_OCTANTS = 96
 CODE_SHIFT = 191.0
 EMPTY_CODE = -1000.0
+PRESSURE_SPANS = (((0, 4), (4, 8)), ((0, 8),))
 LAYER = 128
+
+
+def far_first(across):
+    ring = (2, 1, 3, 0)
+    along_y = (2, 1) if across else (0, 1)
+    shifts = [(z, x, y) for z in ring for x in ring for y in range(2)]
+    return sorted(shifts, key=lambda s: -(min(s[0], 4 - s[0]) + min(s[1], 4 - s[1]) + along_y[s[2]]))
 
 
 def phase(name):
@@ -186,6 +194,11 @@
     def _():
         greet(grp, blk + 1)
 
+    def column_at(shift):
+        z, x, y = blk // 8 + shift[0], blk // 2 + shift[1], blk + shift[2]
+        return lax.rem(z, 4) * 8 + lax.rem(x, 4) * 2 + lax.rem(y, 2)
+
+    columns = {shift: column_at(shift) for shift in far_first(True)}
     beside = jnp.where(has_below, 1, 0) + jnp.where(has_above, 1, 0)
 
     def send(src, dst, send_sem, recv_sem, g, c):
@@ -250,19 +263,6 @@
             k == 0, fill_below, jnp.where(k == 7, fill_above, 0.0)
         )
 
-        with phase("m_barrier"):
-            pl.semaphore_wait(barrier, n_blk + beside)
-
-        mine = grp * n_blk + blk
-
-        def send_octants(it, carry):
-            c = lax.rem(blk + 11 * grp + it, n_blk)
-            send(oct_send.at[c], oct_in.at[mine], oct_send_sem, oct_sem, n_mech, c)
-            return carry
-
-        with phase("m_send_oct"):
-            lax.fori_loop(0, n_blk, send_octants, 0)
-
         @pl.when(jnp.logical_not(has_below))
         def _():
             fill_in[0] = jnp.zeros((8, LANES), F32)
@@ -274,9 +274,6 @@
             fill_in[1] = jnp.zeros((8, LANES), F32)
             for step in range(STEPS):
                 face_in[step, 1] = jnp.zeros((192, LANES), F32)
-
-        with phase("m_load"):
-            loads[0].wait()
 
         def dilate(i, carry):
             f = gradients(cur, i)
@@ -287,7 +284,7 @@
             )
             change = (det - 1.0) * filled * DILATION_SCALE
             for j in range(8):
-                dil_rows[pl.ds(i * 8 + j, 8, stride=64), :] = change[j]
+                dil_rows[pl.ds(i * 64 + j, 8, stride=8), :] = change[j]
             return carry
 
         def elastic(i, carry):
@@ -308,7 +305,11 @@
             for r in range(3):
                 p = [f[r][0] * s[0][j] + f[r][1] * s[1][j] + f[r][2] * s[2][j] for j in range(3)]
                 put_slab(piola, r, i, p[0])
-                put_slab(part, r, i, along_j(p[1]) + along_k(p[2]))
+                own = slab(cur, r, i)
+                z_below = pltpu.roll(pltpu.roll(own, 1, 1), 1, 2)
+                z_above = pltpu.roll(pltpu.roll(own, 7, 1), LANES - 1, 2)
+                pull = k_weight * (jnp.where(iota(own.shape, 1) == 0, z_below, z_above) - own)
+                put_slab(part, r, i, along_j(p[1]) + along_k(p[2]) + pull)
             cof = cofactors(f)
             for r in range(3):
                 for j in range(3):
@@ -317,7 +318,7 @@
 
         def swell(i, carry):
             pressure = jnp.concatenate(
-                [press[pl.ds(i * 8 + j, 8, stride=64), :][None] for j in range(8)], axis=0
+                [press[pl.ds(i * 64 + j, 8, stride=8), :][None] for j in range(8)], axis=0
             )
             for r in range(3):
                 p = [pressure * slab(cofactor, 3 * r + j, i) for j in range(3)]
@@ -328,68 +329,38 @@
         def advance(i, carry):
             below, above, scale = i_span(i)
             gain = (TIME_STEP / UNIT_LENGTH) * slab(mat, 2, i) * filled
-            at_first = iota((8, 8, LANES), 1) == 0
             for r in range(3):
                 s = slab(cur, r, i)
                 force = slab(part, r, i) + (slab(piola, r, above) - slab(piola, r, below)) * scale
-                z_below = pltpu.roll(pltpu.roll(s, 1, 1), 1, 2)
-                z_above = pltpu.roll(pltpu.roll(s, 7, 1), LANES - 1, 2)
-                force = force + k_weight * (jnp.where(at_first, z_below, z_above) - s)
                 put_slab(cur, r, i, s + gain * force)
             return carry
 
-        for step in range(STEPS):
-            with phase("m_dilate"):
-                lax.fori_loop(0, 8, dilate, 0)
-            if step > 0:
-                wait_all(dil_send, dil_send_sem.at[step - 1])
-            with phase("m_take"):
-                taken = lax.dot_general(
-                    perm[...],
-                    dil_rows[...].astype(BF16),
-                    (((1,), (1,)), ((), ())),
-                    preferred_element_type=F32,
-                )
-                dil_send[...] = taken.reshape(n_blk, CAP, NODES).astype(BF16)
-
-            def send_dilation(it, carry):
-                c = lax.rem(blk + 11 * grp + it, n_blk)
+        def take(first, last):
+            lanes = slice(first * 64, last * 64)
+            lax.fori_loop(first, last, dilate, 0)
+            taken = lax.dot_general(
+                perm[...],
+                dil_rows[lanes, :].astype(BF16),
+                (((1,), (1,)), ((), ())),
+                preferred_element_type=F32,
+            )
+            dil_send[:, :, lanes] = taken.reshape(n_blk, CAP, (last - first) * 64).astype(BF16)
+
+        def send_taken(step, first, last):
+            lanes = pl.ds(first * 64, (last - first) * 64)
+
+            for shift in far_first(True):
+                c = columns[shift]
                 send(
-                    dil_send.at[c],
-                    dil_in.at[step, mine],
+                    dil_send.at[c, :, lanes],
+                    dil_in.at[step, mine, :, lanes],
                     dil_send_sem.at[step],
-                    dil_sem.at[step],
+                    dil_sem.at[step, grp],
                     n_mech,
                     c,
                 )
-                return carry
-
-            with phase("m_send_dil"):
-                lax.fori_loop(0, n_blk, send_dilation, 0)
-            if step == 0:
-
-                @pl.when(has_above)
-                def _():
-                    send(
-                        fill_send,
-                        fill_in.at[0],
-                        fill_send_sem.at[1],
-                        fill_sem.at[0],
-                        grp,
-                        blk + 1,
-                    )
-
-                @pl.when(has_below)
-                def _():
-                    send(
-                        fill_send,
-                        fill_in.at[1],
-                        fill_send_sem.at[0],
-                        fill_sem.at[1],
-                        grp,
-                        blk - 1,
-                    )
-
+
+        def send_faces(step):
             for r in range(3):
 
                 @pl.when(has_above)
@@ -413,37 +384,85 @@
                         grp,
                         blk - 1,
                     )
-            if step == 0:
-                loads[1].wait()
+
+        with phase("m_load"):
+            loads[0].wait()
+        with phase("m_take"):
+            take(0, 8)
+
+        with phase("m_barrier"):
+            pl.semaphore_wait(barrier, n_blk + beside)
+
+        mine = grp * n_blk + blk
+
+        with phase("m_send_oct"):
+            for shift in far_first(True):
+                c = columns[shift]
+                send(oct_send.at[c], oct_in.at[mine], oct_send_sem, oct_sem, n_mech, c)
+
+        loads[1].wait()
+        for step in range(STEPS):
             with phase("m_elastic"):
                 lax.fori_loop(0, 8, elastic, 0)
-            with phase("m_wait_press"):
-                wait_all(press_in.at[step], press_sem.at[step])
-            with phase("m_press"):
-                arrived = press_in[step].astype(F32).reshape(slots, NODES).astype(BF16)
-                press[...] = PRESSURE_SCALE * lax.dot_general(
-                    arrived, perm[...], (((0,), (0,)), ((), ())), preferred_element_type=F32
-                )
-            with phase("m_swell"):
-                lax.fori_loop(0, 8, swell, 0)
-            for side, present in ((0, has_below), (1, has_above)):
-
-                @pl.when(present)
+            if step == 0:
+                with phase("m_send_dil"):
+                    send_taken(0, 0, 8)
+
+                @pl.when(has_above)
                 def _():
-                    wait_all(face_in.at[step, side], face_sem.at[step, side])
-                    wait_all(face_in.at[step, side], face_send_sem.at[step, side])
-                    if step == 0:
-                        wait_all(fill_send, fill_sem.at[side])
-                        wait_all(fill_send, fill_send_sem.at[side])
-
-                at = 7 * side
-                weight = (PENALTY * UNIT_LENGTH) * fill_in[side]
-                for r in range(3):
-                    other = face_in[step, side, pl.ds(r * 64, 64), :].reshape(8, 8, LANES)
-                    extra = weight * (other - slab(cur, r, at))
-                    put_slab(part, r, at, slab(part, r, at) + extra)
-            with phase("m_advance"):
-                lax.fori_loop(0, 8, advance, 0)
+                    send(fill_send, fill_in.at[0], fill_send_sem.at[1], fill_sem.at[0], grp, blk + 1)
+
+                @pl.when(has_below)
+                def _():
+                    send(fill_send, fill_in.at[1], fill_send_sem.at[0], fill_sem.at[1], grp, blk - 1)
+
+                send_faces(0)
+            with phase("m_faces"):
+                for side, present in ((0, has_below), (1, has_above)):
+
+                    @pl.when(present)
+                    def _():
+                        wait_all(face_in.at[step, side], face_sem.at[step, side])
+                        wait_all(face_in.at[step, side], face_send_sem.at[step, side])
+                        if step == 0:
+                            wait_all(fill_send, fill_sem.at[side])
+                            wait_all(fill_send, fill_send_sem.at[side])
+
+                    at = 7 * side
+                    weight = (PENALTY * UNIT_LENGTH) * fill_in[side]
+                    for r in range(3):
+                        other = face_in[step, side, pl.ds(r * 64, 64), :].reshape(8, 8, LANES)
+                        extra = weight * (other - slab(cur, r, at))
+                        put_slab(part, r, at, slab(part, r, at) + extra)
+            for at, (first, last) in enumerate(PRESSURE_SPANS[step]):
+                lanes = slice(first * 64, last * 64)
+                with phase("m_wait_press"):
+                    wait_all(
+                        press_in.at[step, :, :, pl.ds(first * 64, (last - first) * 64)],
+                        press_sem.at[step, at],
+                    )
+                with phase("m_press"):
+                    arrived = press_in[step, :, :, lanes].astype(F32)
+                    press[lanes, :] = PRESSURE_SCALE * lax.dot_general(
+                        arrived.reshape(slots, (last - first) * 64).astype(BF16),
+                        perm[...],
+                        (((0,), (0,)), ((), ())),
+                        preferred_element_type=F32,
+                    )
+                with phase("m_swell"):
+                    lax.fori_loop(first, last, swell, 0)
+                with phase("m_advance"):
+                    lax.fori_loop(max(first - 1, 0), last - 1 if last < 8 else 8, advance, 0)
+                if step + 1 < STEPS:
+                    if at == 0:
+                        wait_all(dil_send, dil_send_sem.at[step])
+                    ready = (max(first - 2, 0), last - 2 if last < 8 else 8)
+                    with phase("m_take"):
+                        take(*ready)
+                    with phase("m_send_dil"):
+                        send_taken(step + 1, *ready)
+            if step + 1 < STEPS:
+                send_faces(step + 1)
         wait_all(oct_send, oct_send_sem)
         wait_all(dil_send, dil_send_sem.at[STEPS - 1])
 
@@ -451,35 +470,32 @@
         with phase("s_greet"):
             for g in range(n_mech):
 
-                def greet_element(it, carry):
-                    greet(g, lax.rem(blk + 11 * g + it, n_blk))
-                    return carry
-
-                lax.fori_loop(0, n_blk, greet_element, 0)
+                for shift in far_first(g < 2):
+                    greet(g, columns[shift])
         row = iota((768, LANES), 0)
         at_octant = row // 8 == iota((768, LANES), 1)
         for k in range(8):
             select[:, k * LANES : (k + 1) * LANES] = flag(at_octant & (row % 8 == k), BF16)
-        def split(value, lanes):
+        def split(value, lanes, parts):
             count = value.shape[0]
             high = value.astype(BF16)
             rest = value - high.astype(F32)
             middle = rest.astype(BF16)
             low = (rest - middle.astype(F32)).astype(BF16)
-            for at, piece in enumerate((high, middle, low)):
+            for at, piece in enumerate((high, middle, low)[0:parts]):
                 pieces[at * count : (at + 1) * count, lanes] = piece
 
-        def joined(product):
-            count = product.shape[0] // 3
-            return product[0:count] + product[count : 2 * count] + product[2 * count : 3 * count]
+        def joined(product, parts):
+            count = product.shape[0] // parts
+            return sum(product[at * count : (at + 1) * count] for at in range(parts))
 
         def to_layers(source, target, first, scale):
             for zq in range(6):
-                split(source[pl.ds(zq, 256, stride=6), :], slice(zq * LANES, zq * LANES + LANES))
+                split(source[pl.ds(zq, 256, stride=6), :], slice(zq * LANES, zq * LANES + LANES), 3)
             for pair in range(4):
                 lanes = slice(pair * 256, pair * 256 + 256)
                 both = joined(
-                    jnp.dot(pieces[:, 0:768], select[:, lanes], preferred_element_type=F32)
+                    jnp.dot(pieces[:, 0:768], select[:, lanes], preferred_element_type=F32), 3
                 )
                 for half in range(2):
                     value = scale * both[:, half * LANES : (half + 1) * LANES]
@@ -495,15 +511,16 @@
                     for start, last in spans
                     for at in [((first + x) * 8 + k) * 16 for x in range(start, last)]
                 ]
-                split(jnp.concatenate(rows, axis=0), slice(k * LANES, (k + 1) * LANES))
+                split(jnp.concatenate(rows, axis=0), slice(k * LANES, (k + 1) * LANES), 2)
             for pair in range(3):
                 both = joined(
                     lax.dot_general(
-                        pieces[0 : 3 * count, :],
+                        pieces[0 : 2 * count, :],
                         select[pair * 256 : pair * 256 + 256, :],
                         (((1,), (1,)), ((), ())),
                         preferred_element_type=F32,
-                    )
+                    ),
+                    2,
                 )
                 for half in range(2):
                     taken = 0
@@ -514,9 +531,6 @@
                         ]
                         taken += more
 
-        def half_weight(v):
-            return 0.25 + 0.5 * v * v
-
         plane = (1, 16, LANES)
         not_first = flag(iota(plane, 1) > 0)
         not_last = flag(iota(plane, 1) < 15)
@@ -530,35 +544,40 @@
             def rows_from(row):
                 return source[pl.ds(row, LAYER), :].reshape(8, 16, LANES)
 
+            below = rows_from((source_first - 1) * LAYER)
+            first = rows_from(source_first * LAYER)
+            entering = (below * below + (first * first + 1.0)) * (first - below)
+
             def one_layer(x, carry):
+                centre, entering = carry
                 row = pl.multiple_of((source_first + x) * LAYER, LAYER)
-                centre = rows_from(row)
-                x_below = rows_from(pl.multiple_of(row - LAYER, LAYER))
                 x_above = rows_from(pl.multiple_of(row + LAYER, LAYER))
                 y_below, y_above = rows_from(row - 1), rows_from(row + 1)
-                weight = half_weight(centre)
+                square = centre * centre
+                weight = square + 1.0
 
                 def flux(there):
-                    return (weight + half_weight(there)) * (there - centre)
-
-                inflow = flux(x_above) + flux(x_below)
+                    return (weight + there * there) * (there - centre)
+
+                leaving = flux(x_above)
+                inflow = leaving - entering
                 inflow = inflow + not_last * flux(y_above) + not_first * flux(y_below)
                 after = jnp.where(at_end, centre[7:8], pltpu.roll(centre[0:1], LANES - 1, 2))
                 before = jnp.where(at_start, centre[0:1], pltpu.roll(centre[7:8], 1, 2))
-                inner = (weight[1:] + weight[:-1]) * (centre[1:] - centre[:-1])
-                leave = (weight[7:8] + half_weight(after)) * (after - centre[7:8])
-                enter = (weight[0:1] + half_weight(before)) * (before - centre[0:1])
+                inner = (weight[1:] + square[:-1]) * (centre[1:] - centre[:-1])
+                leave = (weight[7:8] + after * after) * (after - centre[7:8])
+                enter = (weight[0:1] + before * before) * (before - centre[0:1])
                 inflow = inflow + (
                     jnp.concatenate([inner, leave], axis=0)
-                    + jnp.concatenate([enter, -inner], axis=0)
+                    - jnp.concatenate([-enter, inner], axis=0)
                 )
                 gain = rows_of(diff, (diff_first + x) * LAYER, LAYER).reshape(8, 16, LANES)
                 updated = centre + gain * inflow
                 at = pl.multiple_of((target_first + x) * LAYER, LAYER)
                 target[pl.ds(at, LAYER), :] = updated.reshape(LAYER, LANES)
-                return carry
-
-            lax.fori_loop(0, last - start, one_layer, 0)
+                return x_above, leaving
+
+            lax.fori_loop(0, last - start, one_layer, (first, entering))
 
         with phase("s_load"):
             loads[0].wait()
@@ -568,50 +587,75 @@
         def make_pressure(step):
             phi = phi_a.at[step]
 
-            def one_k(k, carry):
+            def one_i(i, carry):
                 for t in range(4):
                     x, y = 8 * (t // 2), 8 * (t % 2)
                     value = jnp.concatenate(
-                        [rows_of(phi, ((2 + x + i) * 8 + k) * 16 + y, 8) for i in range(8)], axis=0
+                        [rows_of(phi, ((2 + x + i) * 8 + k) * 16 + y, 8) for k in range(8)], axis=0
                     )
                     value = value + CUBIC_TERM * value * value * value
-                    at = pl.multiple_of(k * 64, 64)
+                    at = pl.multiple_of(i * 64, 64)
                     pi_rows[pl.ds(at, 64), t * LANES : (t + 1) * LANES] = value.astype(BF16)
                 return carry
 
-            lax.fori_loop(0, 8, one_k, 0)
+            lax.fori_loop(0, 8, one_i, 0)
 
         def send_pressure(step):
-            for g in range(n_mech):
-                rows = slice(g * n_blk * CAP, (g + 1) * n_blk * CAP)
-                taken = lax.dot_general(
-                    hits[rows, :],
-                    pi_rows[...],
-                    (((1,), (1,)), ((), ())),
-                    preferred_element_type=F32,
-                )
-                press_send[step, g * n_blk : (g + 1) * n_blk] = taken.reshape(
-                    n_blk, CAP, NODES
-                ).astype(BF16)
-
-                def send_one(it, carry):
-                    c = lax.rem(blk + 11 * g + it, n_blk)
-                    send(
-                        press_send.at[step, g * n_blk + c],
-                        press_in.at[step, blk],
-                        press_send_sem.at[step],
-                        press_sem.at[step],
-                        g,
-                        c,
+            for at, (first, last) in enumerate(PRESSURE_SPANS[step]):
+                wide = slice(first * 64, last * 64)
+                lanes = pl.ds(first * 64, (last - first) * 64)
+                for g in range(n_mech):
+                    taken = lax.dot_general(
+                        hits[g * n_blk * CAP : (g + 1) * n_blk * CAP, :],
+                        pi_rows[wide, :],
+                        (((1,), (1,)), ((), ())),
+                        preferred_element_type=F32,
                     )
-                    return carry
-
-                lax.fori_loop(0, n_blk, send_one, 0)
+                    press_send[step, g * n_blk : (g + 1) * n_blk, :, wide] = taken.reshape(
+                        n_blk, CAP, (last - first) * 64
+                    ).astype(BF16)
+
+                    for shift in far_first(g < 2):
+                        c = columns[shift]
+                        send(
+                            press_send.at[step, g * n_blk + c, :, lanes],
+                            press_in.at[step, blk, :, lanes],
+                            press_send_sem.at[step],
+                            press_sem.at[step, at],
+                            g,
+                            c,
+                        )
 
         with phase("s_pi"):
             make_pressure(0)
+        loads[1].wait()
+        with phase("s_to_layers_d"):
+            to_layers(mat, diff, 1, 0.5 * SWEEP_STEP)
         with phase("s_barrier"):
             pl.semaphore_wait(barrier, beside)
+
+        @pl.when(has_above)
+        def _():
+            send(
+                diff.at[pl.ds(16 * LAYER, LAYER)],
+                diff.at[pl.ds(0, LAYER)],
+                rim_send_sem.at[1],
+                rim_sem.at[0],
+                grp,
+                blk + 1,
+            )
+
+        @pl.when(has_below)
+        def _():
+            send(
+                diff.at[pl.ds(LAYER, LAYER)],
+                diff.at[pl.ds(17 * LAYER, LAYER)],
+                rim_send_sem.at[0],
+                rim_sem.at[1],
+                grp,
+                blk - 1,
+            )
+
         with phase("s_wait_oct"):
             wait_all(oct_in, oct_sem)
         with phase("s_hits"):
@@ -631,32 +675,6 @@
                 hits[:, t * LANES : (t + 1) * LANES] = flag(mine, BF16)
         with phase("s_send_press"):
             send_pressure(0)
-        loads[1].wait()
-        with phase("s_to_layers_d"):
-            to_layers(mat, diff, 1, SWEEP_STEP)
-
-        @pl.when(has_above)
-        def _():
-            send(
-                diff.at[pl.ds(16 * LAYER, LAYER)],
-                diff.at[pl.ds(0, LAYER)],
-                rim_send_sem.at[1],
-                rim_sem.at[0],
-                grp,
-                blk + 1,
-            )
-
-        @pl.when(has_below)
-        def _():
-            send(
-                diff.at[pl.ds(LAYER, LAYER)],
-                diff.at[pl.ds(17 * LAYER, LAYER)],
-                rim_send_sem.at[0],
-                rim_sem.at[1],
-                grp,
-                blk - 1,
-            )
-
         @pl.when(jnp.logical_not(has_below))
         def _():
             diff[0:LAYER, :] = jnp.zeros((LAYER, LANES), F32)
@@ -676,29 +694,52 @@
                     make_pressure(step)
                 with phase("s_send_press"):
                     send_pressure(step)
-            with phase("s_wait_dil"):
-                wait_all(dil_in.at[step], dil_sem.at[step])
-            with phase("s_deposit"):
-                arrived = dil_in[step].astype(F32).reshape(n_mech * n_blk * CAP, NODES).astype(BF16)
-                total[...] = lax.dot_general(
-                    arrived, hits[...], (((0,), (0,)), ((), ())), preferred_element_type=F32
+            for g in (2, 0, 1):
+                span = slice(g * n_blk, (g + 1) * n_blk)
+                rows = slice(g * n_blk * CAP, (g + 1) * n_blk * CAP)
+                with phase("s_wait_dil"):
+                    wait_all(dil_in.at[step, span], dil_sem.at[step, g])
+                arrived = dil_in[step, span].astype(F32)
+                arrived = arrived.reshape(n_blk * CAP, NODES).astype(BF16)
+                if g != 1:
+                    with phase("s_collect"):
+                        share = lax.dot_general(
+                            arrived,
+                            hits[rows, :],
+                            (((0,), (0,)), ((), ())),
+                            preferred_element_type=F32,
+                        )
+                        total[...] = share if g == 2 else total[...] + share
+
+            def finish(ox, first, last):
+                taken = slice(first * 64, last * 64)
+                lanes = slice(ox * 256, ox * 256 + 256)
+                total[taken, lanes] = total[taken, lanes] + lax.dot_general(
+                    arrived[:, taken],
+                    hits[rows, lanes],
+                    (((0,), (0,)), ((), ())),
+                    preferred_element_type=F32,
                 )
 
-                def one_k(k, carry):
-                    for t in range(4):
-                        for i in range(8):
-                            x, y = 8 * (t // 2) + i, 8 * (t % 2)
-                            at = pl.multiple_of(((2 + x) * 8 + k) * 16 + y, 8)
+                def one_i(i, carry):
+                    for oy in range(2):
+                        for k in range(8):
+                            at = pl.multiple_of(((2 + 8 * ox + i) * 8 + k) * 16 + 8 * oy, 8)
+                            octant = 2 * ox + oy
                             more = total[
-                                pl.ds(pl.multiple_of(k * 64 + i * 8, 8), 8),
-                                t * LANES : (t + 1) * LANES,
+                                pl.ds(pl.multiple_of(i * 64 + k * 8, 8), 8),
+                                octant * LANES : (octant + 1) * LANES,
                             ]
                             phi[pl.ds(at, 8), :] = (
                                 phi[pl.ds(at, 8), :] + (SWEEP_STEP * SOURCE_RATE) * more
                             )
                     return carry
 
-                lax.fori_loop(0, 8, one_k, 0)
+                lax.fori_loop(first, last, one_i, 0)
+
+            with phase("s_deposit_edge"):
+                finish(0, 0, 2)
+                finish(1, 6, 8)
 
             @pl.when(has_above)
             def _():
@@ -722,6 +763,9 @@
                     blk - 1,
                 )
 
+            with phase("s_deposit"):
+                finish(0, 2, 8)
+                finish(1, 0, 6)
             after = phi_a.at[(step + 1) % 2]
             with phase("s_sweep_inner"):
                 sweep(phi, 2, phi_b, 1, 1, 1, 15)
@@ -806,9 +850,9 @@
             dma,
             dma,
             dma((STEPS,)),
+            dma((STEPS, n_mech)),
             dma((STEPS,)),
-            dma((STEPS,)),
-            dma((STEPS,)),
+            dma((STEPS, 2)),
             dma((STEPS, 2)),
             dma((STEPS, 2)),
             dma((2,)),

time: 43.7 us -> 40.7 us (0.931); the launches traced: 43.5 us -> 40 us
  Pallas kernels: 42 us -> 38.4 us
    pallas_call x1, Pallas kernels: 42 us -> 38.4 us  [shards(): call(state.reshape(whole), material.reshape(whole), occupied.reshape(1, L...]
where the time goes in v2:
time: 40.7 us; the launch traced here: 40 us
  Pallas kernels  38.4 us (94%)
  local copies, waits for them, and re-layouts  1.56 us (4%)
    pallas_call x1, Pallas kernels, shards(): call(state.reshape(whole), material.reshape(whole), occupied.reshape(1, L...  38.4 us
    unnamed x7, local copies, waits for them, and re-layouts  1.56 us

profile of v2, /device:TPU:49, one launch (start us, length us, event | category | flops | bytes accessed | tf_op | source)
XLA Modules:
  0.0 40.0 jit_solution(3219885294984926633)
XLA Ops:
  0.0 0.0 copy-start
  0.0 0.0 copy-start.1
  0.0 0.0 copy-start.2
  0.0 0.6 %copy-done = s32[128]{0:T(128)S(1)} copy-done((s32[128]{0:T(128)S(1)}, s32[128]{0:T(128)}, u32[]{:S(2)}) %copy-start) | copy-done | bytes 536
  0.7 0.0 copy-done.1
  0.7 0.0 copy-done.2
  0.7 38.4 %shard_map.55 = f32[1536,128]{1,0:T(8,128)S(1)} custom-call(f32[1536,128]{1,0:T(8,128)} %bitcast.10, f32[1536,128]{1,0:T(8,128)} %bitcast.11, s32[1,128]{1,0:T(1,128)S(1)} %bitcast.7, s32[1,128]{1,0:T(1,128)S(1)} %bitcast.8, s32[1,128]{1,0:T(1,128)S(1)} %bitcast.9), custom_call_target="tpu_custom_call" | custom-call | tf_op jit(solution)/shard_map/pallas_call | solution.py:871
  39.1 0.9 %copy.7 = f32[1,3,512,128]{3,2,1,0:T(8,128)} copy(f32[1,3,512,128]{3,2,1,0:T(8,128)S(1)} %bitcast.6) | data formatting | bytes 1572864
Async XLA Ops:
  0.0 0.7 %copy-start = (s32[128]{0:T(128)S(1)}, s32[128]{0:T(128)}, u32[]{:S(2)}) copy-start(s32[128]{0:T(128)} %param.7) | copy-start | bytes 1540
  0.0 0.7 %copy-start.1 = (s32[128,1]{0,1:T(1,128)S(1)}, s32[128,1]{0,1:T(1,128)}, u32[]{:S(2)}) copy-start(s32[128,1]{0,1:T(1,128)} %param.8) | copy-start | bytes 1540
  0.0 0.7 %copy-start.2 = (s32[128]{0:T(128)S(1)}, s32[128]{0:T(128)}, u32[]{:S(2)}) copy-start(s32[128]{0:T(128)} %param.9) | copy-start | bytes 1540

commit v3 on v2

--- a/solution.py
+++ b/solution.py
@@ -24,10 +24,11 @@
 LANES = 128
 NODES = 512
 CAP = 8
+HALO_PIECE = 64
 DEPTH_OCTANTS = 96
 CODE_SHIFT = 191.0
 EMPTY_CODE = -1000.0
-PRESSURE_SPANS = (((0, 4), (4, 8)), ((0, 8),))
+PRESSURE_SPANS = (((0, 4), (4, 6), (6, 8)), ((0, 8),))
 LAYER = 128
 
 
@@ -50,12 +51,16 @@
     return jnp.where(mask, 1.0, 0.0).astype(dtype)
 
 
+def aligned(start, count):
+    return start if isinstance(start, int) else pl.multiple_of(start, count)
+
+
 def wait_all(ref, sem):
     pltpu.make_async_copy(ref, ref, sem).wait()
 
 
 def rows_of(ref, start, count):
-    return ref[pl.ds(pl.multiple_of(start, count), count), :]
+    return ref[pl.ds(aligned(start, count), count), :]
 
 
 def slab(ref, r, i):
@@ -63,7 +68,7 @@
 
 
 def put_slab(ref, r, i, value):
-    ref[pl.ds(pl.multiple_of(r * 512 + i * 64, 64), 64), :] = value.reshape(64, LANES)
+    ref[pl.ds(aligned(r * 512 + i * 64, 64), 64), :] = value.reshape(64, LANES)
 
 
 def along_j(s):
@@ -79,6 +84,8 @@
 
 
 def i_span(i):
+    if isinstance(i, int):
+        return max(i - 1, 0), min(i + 1, 7), 1.0 if i in (0, 7) else 0.5
     below, above = jnp.maximum(i - 1, 0), jnp.minimum(i + 1, 7)
     return below, above, jnp.where((i == 0) | (i == 7), 1.0, 0.5)
 
@@ -152,33 +159,25 @@
     phi_a,
     phi_b,
     diff,
+    halo_send,
+    halo_in,
+    pick,
+    packed,
     pi_rows,
     total,
-    load_sem,
-    small_sem,
-    oct_send_sem,
-    oct_sem,
-    dil_send_sem,
-    dil_sem,
-    press_send_sem,
-    press_sem,
-    face_send_sem,
-    face_sem,
-    fill_send_sem,
-    fill_sem,
-    halo_send_sem,
-    halo_sem,
-    rim_send_sem,
-    rim_sem,
+    local_sem,
+    send_sem,
+    recv_sem,
 ):
     grp, blk = lax.axis_index("grp"), lax.axis_index("blk")
+    sent, got = send_sem, recv_sem
     n_mech = n_grp - 1
     solvent = grp == n_mech
     barrier = pltpu.get_barrier_semaphore()
     has_below, has_above = blk > 0, blk < n_blk - 1
     loads = [
-        pltpu.make_async_copy(state_ref, cur, load_sem.at[0]),
-        pltpu.make_async_copy(material_ref, mat, load_sem.at[1]),
+        pltpu.make_async_copy(state_ref, cur, local_sem.at[0]),
+        pltpu.make_async_copy(material_ref, mat, local_sem.at[1]),
     ]
     for copy in loads:
         copy.start()
@@ -212,9 +211,20 @@
         )
         copy.start()
 
+    def send_pieces(source, first, target, there, count, send_sem, recv_sem, g, c):
+        for at in range(0, count, HALO_PIECE):
+            send(
+                source.at[pl.ds(first + at, HALO_PIECE)],
+                target.at[pl.ds(there + at, HALO_PIECE)],
+                send_sem,
+                recv_sem,
+                g,
+                c,
+            )
+
     def mechanics():
         small = [
-            pltpu.make_async_copy(source, target, small_sem.at[at])
+            pltpu.make_async_copy(source, target, local_sem.at[2 + at])
             for at, (source, target) in enumerate(
                 (
                     (occupied_ref, occupied_in),
@@ -337,7 +347,8 @@
 
         def take(first, last):
             lanes = slice(first * 64, last * 64)
-            lax.fori_loop(first, last, dilate, 0)
+            for i in range(first, last):
+                dilate(i, 0)
             taken = lax.dot_general(
                 perm[...],
                 dil_rows[lanes, :].astype(BF16),
@@ -354,8 +365,8 @@
                 send(
                     dil_send.at[c, :, lanes],
                     dil_in.at[step, mine, :, lanes],
-                    dil_send_sem.at[step],
-                    dil_sem.at[step, grp],
+                    sent.at[1 + step],
+                    got.at[1 + n_mech * step + grp],
                     n_mech,
                     c,
                 )
@@ -368,8 +379,8 @@
                     send(
                         cur.at[pl.ds(r * 512 + 448, 64)],
                         face_in.at[step, 0, pl.ds(r * 64, 64)],
-                        face_send_sem.at[step, 1],
-                        face_sem.at[step, 0],
+                        sent.at[3 + 2 * step + 1],
+                        got.at[4 + 2 * step + 0],
                         grp,
                         blk + 1,
                     )
@@ -379,8 +390,8 @@
                     send(
                         cur.at[pl.ds(r * 512, 64)],
                         face_in.at[step, 1, pl.ds(r * 64, 64)],
-                        face_send_sem.at[step, 0],
-                        face_sem.at[step, 1],
+                        sent.at[3 + 2 * step + 0],
+                        got.at[4 + 2 * step + 1],
                         grp,
                         blk - 1,
                     )
@@ -398,8 +409,17 @@
         with phase("m_send_oct"):
             for shift in far_first(True):
                 c = columns[shift]
-                send(oct_send.at[c], oct_in.at[mine], oct_send_sem, oct_sem, n_mech, c)
-
+                send(oct_send.at[c], oct_in.at[mine], sent.at[0], got.at[0], n_mech, c)
+
+        @pl.when(has_above)
+        def _():
+            send(fill_send, fill_in.at[0], sent.at[7 + 1], got.at[8 + 0], grp, blk + 1)
+
+        @pl.when(has_below)
+        def _():
+            send(fill_send, fill_in.at[1], sent.at[7 + 0], got.at[8 + 1], grp, blk - 1)
+
+        send_faces(0)
         loads[1].wait()
         for step in range(STEPS):
             with phase("m_elastic"):
@@ -407,26 +427,18 @@
             if step == 0:
                 with phase("m_send_dil"):
                     send_taken(0, 0, 8)
-
-                @pl.when(has_above)
-                def _():
-                    send(fill_send, fill_in.at[0], fill_send_sem.at[1], fill_sem.at[0], grp, blk + 1)
-
-                @pl.when(has_below)
-                def _():
-                    send(fill_send, fill_in.at[1], fill_send_sem.at[0], fill_sem.at[1], grp, blk - 1)
-
-                send_faces(0)
+            if step > 0:
+                send_faces(step)
             with phase("m_faces"):
                 for side, present in ((0, has_below), (1, has_above)):
 
                     @pl.when(present)
                     def _():
-                        wait_all(face_in.at[step, side], face_sem.at[step, side])
-                        wait_all(face_in.at[step, side], face_send_sem.at[step, side])
+                        wait_all(face_in.at[step, side], got.at[4 + 2 * step + side])
+                        wait_all(face_in.at[step, side], sent.at[3 + 2 * step + side])
                         if step == 0:
-                            wait_all(fill_send, fill_sem.at[side])
-                            wait_all(fill_send, fill_send_sem.at[side])
+                            wait_all(fill_send, got.at[8 + side])
+                            wait_all(fill_send, sent.at[7 + side])
 
                     at = 7 * side
                     weight = (PENALTY * UNIT_LENGTH) * fill_in[side]
@@ -439,7 +451,7 @@
                 with phase("m_wait_press"):
                     wait_all(
                         press_in.at[step, :, :, pl.ds(first * 64, (last - first) * 64)],
-                        press_sem.at[step, at],
+                        got.at[3 * step + at],
                     )
                 with phase("m_press"):
                     arrived = press_in[step, :, :, lanes].astype(F32)
@@ -450,21 +462,21 @@
                         preferred_element_type=F32,
                     )
                 with phase("m_swell"):
-                    lax.fori_loop(first, last, swell, 0)
+                    for i in range(first, last):
+                        swell(i, 0)
                 with phase("m_advance"):
-                    lax.fori_loop(max(first - 1, 0), last - 1 if last < 8 else 8, advance, 0)
+                    for i in range(max(first - 1, 0), last - 1 if last < 8 else 8):
+                        advance(i, 0)
                 if step + 1 < STEPS:
                     if at == 0:
-                        wait_all(dil_send, dil_send_sem.at[step])
+                        wait_all(dil_send, sent.at[1 + step])
                     ready = (max(first - 2, 0), last - 2 if last < 8 else 8)
                     with phase("m_take"):
                         take(*ready)
                     with phase("m_send_dil"):
                         send_taken(step + 1, *ready)
-            if step + 1 < STEPS:
-                send_faces(step + 1)
-        wait_all(oct_send, oct_send_sem)
-        wait_all(dil_send, dil_send_sem.at[STEPS - 1])
+        wait_all(oct_send, sent.at[0])
+        wait_all(dil_send, sent.at[1 + STEPS - 1])
 
     def brick():
         with phase("s_greet"):
@@ -476,26 +488,25 @@
         at_octant = row // 8 == iota((768, LANES), 1)
         for k in range(8):
             select[:, k * LANES : (k + 1) * LANES] = flag(at_octant & (row % 8 == k), BF16)
-        def split(value, lanes, parts):
+        def split(value, lanes):
             count = value.shape[0]
             high = value.astype(BF16)
             rest = value - high.astype(F32)
             middle = rest.astype(BF16)
             low = (rest - middle.astype(F32)).astype(BF16)
-            for at, piece in enumerate((high, middle, low)[0:parts]):
+            for at, piece in enumerate((high, middle, low)):
                 pieces[at * count : (at + 1) * count, lanes] = piece
 
-        def joined(product, parts):
-            count = product.shape[0] // parts
-            return sum(product[at * count : (at + 1) * count] for at in range(parts))
+        def joined(product):
+            return product[0:256] + product[256:512] + product[512:768]
 
         def to_layers(source, target, first, scale):
             for zq in range(6):
-                split(source[pl.ds(zq, 256, stride=6), :], slice(zq * LANES, zq * LANES + LANES), 3)
+                split(source[pl.ds(zq, 256, stride=6), :], slice(zq * LANES, zq * LANES + LANES))
             for pair in range(4):
                 lanes = slice(pair * 256, pair * 256 + 256)
                 both = joined(
-                    jnp.dot(pieces[:, 0:768], select[:, lanes], preferred_element_type=F32), 3
+                    jnp.dot(pieces[...], select[:, lanes], preferred_element_type=F32)
                 )
                 for half in range(2):
                     value = scale * both[:, half * LANES : (half + 1) * LANES]
@@ -503,30 +514,45 @@
                         at = ((first + x) * 8 + 2 * pair + half) * 16
                         target[at : at + 16, :] = value[x * 16 : x * 16 + 16]
 
+        k_row, column_256 = iota((256, 256), 0), iota((256, 256), 1)
+        for block in range(3):
+            k_held = k_row // LANES * 4 + (k_row // 32 + 4 - block) % 4
+            chosen = (k_row % 32 == column_256 // 8) & (k_held == column_256 % 8)
+            pick[block] = flag(chosen, BF16)
+
         def from_layers(source, first, spans):
             count = 16 * sum(last - start for start, last in spans)
-            for k in range(8):
-                rows = [
-                    source[at : at + 16, :]
-                    for start, last in spans
-                    for at in [((first + x) * 8 + k) * 16 for x in range(start, last)]
-                ]
-                split(jnp.concatenate(rows, axis=0), slice(k * LANES, (k + 1) * LANES), 2)
-            for pair in range(3):
-                both = joined(
-                    lax.dot_general(
-                        pieces[0 : 2 * count, :],
-                        select[pair * 256 : pair * 256 + 256, :],
-                        (((1,), (1,)), ((), ())),
-                        preferred_element_type=F32,
-                    ),
-                    2,
+            place = iota((count, LANES), 1) // 32
+            for half in range(2):
+                lanes = slice(half * LANES, (half + 1) * LANES)
+                turned = []
+                for k in range(4 * half, 4 * half + 4):
+                    rows = [
+                        source[at : at + 16, :]
+                        for start, last in spans
+                        for at in [((first + x) * 8 + k) * 16 for x in range(start, last)]
+                    ]
+                    rows = jnp.concatenate(rows, axis=0)
+                    turned.append(pltpu.roll(rows, 32 * (k % 4), 1) if k % 4 else rows)
+                for block in range(3):
+                    value = turned[(3 - block) % 4]
+                    for at in range(3):
+                        value = jnp.where(place == at, turned[(at - block) % 4], value)
+                    high = value.astype(BF16)
+                    packed[block, 0:count, lanes] = high
+                    packed[block, count : 2 * count, lanes] = (
+                        value - high.astype(F32)
+                    ).astype(BF16)
+            for block in range(3):
+                both = jnp.dot(
+                    packed[block, 0 : 2 * count, :], pick[block], preferred_element_type=F32
                 )
+                both = both[0:count] + both[count : 2 * count]
                 for half in range(2):
                     taken = 0
                     for start, last in spans:
                         more = 16 * (last - start)
-                        cur[pl.ds(start * 96 + 2 * pair + half, more, stride=6), :] = both[
+                        cur[pl.ds(start * 96 + 2 * block + half, more, stride=6), :] = both[
                             taken : taken + more, half * LANES : (half + 1) * LANES
                         ]
                         taken += more
@@ -577,7 +603,7 @@
                 target[pl.ds(at, LAYER), :] = updated.reshape(LAYER, LANES)
                 return x_above, leaving
 
-            lax.fori_loop(0, last - start, one_layer, (first, entering))
+            lax.fori_loop(0, last - start, one_layer, (first, entering), unroll=2)
 
         with phase("s_load"):
             loads[0].wait()
@@ -620,8 +646,8 @@
                         send(
                             press_send.at[step, g * n_blk + c, :, lanes],
                             press_in.at[step, blk, :, lanes],
-                            press_send_sem.at[step],
-                            press_sem.at[step, at],
+                            sent.at[step],
+                            got.at[3 * step + at],
                             g,
                             c,
                         )
@@ -636,28 +662,16 @@
 
         @pl.when(has_above)
         def _():
-            send(
-                diff.at[pl.ds(16 * LAYER, LAYER)],
-                diff.at[pl.ds(0, LAYER)],
-                rim_send_sem.at[1],
-                rim_sem.at[0],
-                grp,
-                blk + 1,
-            )
+            rim = (sent.at[6 + 1], got.at[11 + 0])
+            send_pieces(diff, 16 * LAYER, diff, 0, LAYER, *rim, grp, blk + 1)
 
         @pl.when(has_below)
         def _():
-            send(
-                diff.at[pl.ds(LAYER, LAYER)],
-                diff.at[pl.ds(17 * LAYER, LAYER)],
-                rim_send_sem.at[0],
-                rim_sem.at[1],
-                grp,
-                blk - 1,
-            )
+            rim = (sent.at[6 + 0], got.at[11 + 1])
+            send_pieces(diff, LAYER, diff, 17 * LAYER, LAYER, *rim, grp, blk - 1)
 
         with phase("s_wait_oct"):
-            wait_all(oct_in, oct_sem)
+            wait_all(oct_in, got.at[0])
         with phase("s_hits"):
             spread = (n_mech * n_blk, CAP, LANES)
             one_code = jnp.where(
@@ -698,7 +712,7 @@
                 span = slice(g * n_blk, (g + 1) * n_blk)
                 rows = slice(g * n_blk * CAP, (g + 1) * n_blk * CAP)
                 with phase("s_wait_dil"):
-                    wait_all(dil_in.at[step, span], dil_sem.at[step, g])
+                    wait_all(dil_in.at[step, span], got.at[1 + n_mech * step + g])
                 arrived = dil_in[step, span].astype(F32)
                 arrived = arrived.reshape(n_blk * CAP, NODES).astype(BF16)
                 if g != 1:
@@ -714,28 +728,20 @@
             def finish(ox, first, last):
                 taken = slice(first * 64, last * 64)
                 lanes = slice(ox * 256, ox * 256 + 256)
-                total[taken, lanes] = total[taken, lanes] + lax.dot_general(
+                share = lax.dot_general(
                     arrived[:, taken],
                     hits[rows, lanes],
                     (((0,), (0,)), ((), ())),
                     preferred_element_type=F32,
                 )
-
-                def one_i(i, carry):
-                    for oy in range(2):
-                        for k in range(8):
-                            at = pl.multiple_of(((2 + 8 * ox + i) * 8 + k) * 16 + 8 * oy, 8)
-                            octant = 2 * ox + oy
-                            more = total[
-                                pl.ds(pl.multiple_of(i * 64 + k * 8, 8), 8),
-                                octant * LANES : (octant + 1) * LANES,
-                            ]
-                            phi[pl.ds(at, 8), :] = (
-                                phi[pl.ds(at, 8), :] + (SWEEP_STEP * SOURCE_RATE) * more
-                            )
-                    return carry
-
-                lax.fori_loop(first, last, one_i, 0)
+                source = (SWEEP_STEP * SOURCE_RATE) * (total[taken, lanes] + share)
+                for i in range(first, last):
+                    for k in range(8):
+                        at, row = ((2 + 8 * ox + i) * 8 + k) * 16, (i - first) * 64 + k * 8
+                        for oy in range(2):
+                            cells = slice(at + 8 * oy, at + 8 * oy + 8)
+                            more = source[row : row + 8, oy * LANES : (oy + 1) * LANES]
+                            phi[cells, :] = phi[cells, :] + more
 
             with phase("s_deposit_edge"):
                 finish(0, 0, 2)
@@ -743,25 +749,17 @@
 
             @pl.when(has_above)
             def _():
-                send(
-                    phi.at[pl.ds(16 * LAYER, 2 * LAYER)],
-                    phi.at[pl.ds(0, 2 * LAYER)],
-                    halo_send_sem.at[step, 1],
-                    halo_sem.at[step, 0],
-                    grp,
-                    blk + 1,
-                )
+                halo_send[1] = phi[16 * LAYER : 18 * LAYER, :].astype(BF16)
+                halo = (sent.at[2 + 2 * step + 1], got.at[7 + 2 * step + 0])
+                target = halo_in.at[step, 0]
+                send_pieces(halo_send.at[1], 0, target, 0, 2 * LAYER, *halo, grp, blk + 1)
 
             @pl.when(has_below)
             def _():
-                send(
-                    phi.at[pl.ds(2 * LAYER, 2 * LAYER)],
-                    phi.at[pl.ds(18 * LAYER, 2 * LAYER)],
-                    halo_send_sem.at[step, 0],
-                    halo_sem.at[step, 1],
-                    grp,
-                    blk - 1,
-                )
+                halo_send[0] = phi[2 * LAYER : 4 * LAYER, :].astype(BF16)
+                halo = (sent.at[2 + 2 * step + 0], got.at[7 + 2 * step + 1])
+                target = halo_in.at[step, 1]
+                send_pieces(halo_send.at[0], 0, target, 0, 2 * LAYER, *halo, grp, blk - 1)
 
             with phase("s_deposit"):
                 finish(0, 2, 8)
@@ -778,13 +776,14 @@
 
                     @pl.when(present)
                     def _():
-                        two = phi.at[pl.ds(first * LAYER, 2 * LAYER)]
-                        wait_all(two, halo_sem.at[step, side])
-                        wait_all(two, halo_send_sem.at[step, side])
+                        two = halo_in.at[step, side]
+                        wait_all(two, got.at[7 + 2 * step + side])
+                        wait_all(two, sent.at[2 + 2 * step + side])
+                        phi[first * LAYER : (first + 2) * LAYER, :] = two[...].astype(F32)
                         if step == 0:
                             one = diff.at[pl.ds(0, LAYER)]
-                            wait_all(one, rim_sem.at[side])
-                            wait_all(one, rim_send_sem.at[side])
+                            wait_all(one, got.at[11 + side])
+                            wait_all(one, sent.at[6 + side])
 
             with phase("s_sweep_edge"):
                 sweep(phi, 2, phi_b, 1, 1, -1, 1)
@@ -792,7 +791,7 @@
                 sweep(phi_b, 1, after, 2, 1, 0, 2)
                 sweep(phi_b, 1, after, 2, 1, 14, 16)
             with phase("s_sent"):
-                wait_all(press_send.at[step], press_send_sem.at[step])
+                wait_all(press_send.at[step], sent.at[step])
         with phase("s_from_edge"):
             from_layers(phi_a.at[STEPS % 2], 2, [(0, 2), (14, 16)])
 
@@ -839,28 +838,19 @@
             vmem((STEPS, n_mech * n_blk, CAP, NODES), BF16),
             vmem((n_mech * n_blk * CAP, NODES), BF16),
             vmem((768, 1024), BF16),
-            vmem((768, 1024), BF16),
+            vmem((768, 768), BF16),
             vmem((2, 20 * LAYER, LANES), F32),
             vmem((18 * LAYER, LANES), F32),
             vmem((18 * LAYER, LANES), F32),
+            vmem((2, 2 * LAYER, LANES), BF16),
+            vmem((STEPS, 2, 2 * LAYER, LANES), BF16),
+            vmem((3, 256, 256), BF16),
+            vmem((3, 384, 256), BF16),
             vmem((NODES, NODES), BF16),
             vmem((NODES, NODES), F32),
-            dma((2,)),
-            dma((3,)),
-            dma,
-            dma,
-            dma((STEPS,)),
-            dma((STEPS, n_mech)),
-            dma((STEPS,)),
-            dma((STEPS, 2)),
-            dma((STEPS, 2)),
-            dma((STEPS, 2)),
-            dma((2,)),
-            dma((2,)),
-            dma((STEPS, 2)),
-            dma((STEPS, 2)),
-            dma((2,)),
-            dma((2,)),
+            dma((5,)),
+            dma((9,)),
+            dma((13,)),
         ],
         compiler_params=pltpu.CompilerParams(
             collective_id=0, has_side_effects=True, vmem_limit_bytes=55 * 1000000
@@ -868,13 +858,14 @@
     )
 
     def shards(state, material, occupied, brick_column, brick_octant):
-        out = call(
+        operands = (
             state.reshape(whole),
             material.reshape(whole),
             occupied.reshape(1, LANES),
             brick_column.reshape(1, LANES),
             brick_octant.reshape(1, LANES),
         )
+        out = call(*(pltpu.with_memory_space_constraint(x, pltpu.HBM) for x in operands))
         return out.reshape(state.shape)
 
     in_specs = (

time: 40.7 us -> 37.5 us (0.921)
  Pallas kernels: 38.4 us -> 36.1 us
  local copies, waits for them, and re-layouts: 1.56 us -> 0.88 us
    pallas_call x1, Pallas kernels: 38.4 us -> 36.1 us  [shards(): call(*(pltpu.with_memory_space_constraint(x, pltpu.HBM) for x in operands))]
    unnamed x7 -> x1, local copies, waits for them, and re-layouts: 1.56 us -> 0.88 us
where the time goes in v3:
time: 37.5 us; the launch traced here: 37 us
  Pallas kernels  36.1 us (96%)
  local copies, waits for them, and re-layouts  0.88 us (2%)
    pallas_call x1, Pallas kernels, shards(): call(*(pltpu.with_memory_space_constraint(x, pltpu.HBM) for x in operands))  36.1 us
    unnamed x1, local copies, waits for them, and re-layouts  0.88 us

profile of v3, /device:TPU:49, one launch (start us, length us, event | category | flops | bytes accessed | tf_op | source)
XLA Modules:
  0.0 37.0 jit_solution(13619219924136734317)
XLA Ops:
  0.0 36.1 %shard_map.55 = f32[1536,128]{1,0:T(8,128)S(1)} custom-call(f32[1536,128]{1,0:T(8,128)} %bitcast.7, f32[1536,128]{1,0:T(8,128)} %bitcast.8, s32[1,128]{1,0:T(1,128)} %bitcast.9, s32[1,128]{1,0:T(1,128)} %bitcast.10, s32[1,128]{1,0:T(1,128)} %bitcast.11), custom_call_target="tpu_custom_call" | custom-call | tf_op jit(solution)/shard_map/pallas_call | solution.py:868
  36.1 0.9 %copy.7 = f32[1,3,512,128]{3,2,1,0:T(8,128)} copy(f32[1,3,512,128]{3,2,1,0:T(8,128)S(1)} %bitcast.6) | data formatting | bytes 1572864

commit v4 on v3

--- a/solution.py
+++ b/solution.py
@@ -145,6 +145,7 @@
     press_in,
     press,
     face_in,
+    face_send,
     fill_in,
     fill_send,
     piola,
@@ -277,13 +278,13 @@
         def _():
             fill_in[0] = jnp.zeros((8, LANES), F32)
             for step in range(STEPS):
-                face_in[step, 0] = jnp.zeros((192, LANES), F32)
+                face_in[step, 0] = jnp.zeros((192, LANES), BF16)
 
         @pl.when(jnp.logical_not(has_above))
         def _():
             fill_in[1] = jnp.zeros((8, LANES), F32)
             for step in range(STEPS):
-                face_in[step, 1] = jnp.zeros((192, LANES), F32)
+                face_in[step, 1] = jnp.zeros((192, LANES), BF16)
 
         def dilate(i, carry):
             f = gradients(cur, i)
@@ -373,28 +374,39 @@
 
         def send_faces(step):
             for r in range(3):
-
-                @pl.when(has_above)
-                def _():
-                    send(
-                        cur.at[pl.ds(r * 512 + 448, 64)],
-                        face_in.at[step, 0, pl.ds(r * 64, 64)],
-                        sent.at[3 + 2 * step + 1],
-                        got.at[4 + 2 * step + 0],
-                        grp,
-                        blk + 1,
-                    )
-
-                @pl.when(has_below)
-                def _():
-                    send(
-                        cur.at[pl.ds(r * 512, 64)],
-                        face_in.at[step, 1, pl.ds(r * 64, 64)],
-                        sent.at[3 + 2 * step + 0],
-                        got.at[4 + 2 * step + 1],
-                        grp,
-                        blk - 1,
-                    )
+                face_send[0, r * 64 : r * 64 + 64] = cur[r * 512 : r * 512 + 64, :].astype(BF16)
+                face_send[1, r * 64 : r * 64 + 64] = cur[
+                    r * 512 + 448 : r * 512 + 512, :
+                ].astype(BF16)
+
+            @pl.when(has_above)
+            def _():
+                face = (sent.at[3 + 2 * step + 1], got.at[4 + 2 * step + 0])
+                send_pieces(face_send.at[1], 0, face_in.at[step, 0], 0, 192, *face, grp, blk + 1)
+
+            @pl.when(has_below)
+            def _():
+                face = (sent.at[3 + 2 * step + 0], got.at[4 + 2 * step + 1])
+                send_pieces(face_send.at[0], 0, face_in.at[step, 1], 0, 192, *face, grp, blk - 1)
+
+        def meet_faces(step):
+            with phase("m_faces"):
+                for side, present in ((0, has_below), (1, has_above)):
+
+                    @pl.when(present)
+                    def _():
+                        wait_all(face_in.at[step, side], got.at[4 + 2 * step + side])
+                        wait_all(face_in.at[step, side], sent.at[3 + 2 * step + side])
+                        if step == 0:
+                            wait_all(fill_send, got.at[8 + side])
+                            wait_all(fill_send, sent.at[7 + side])
+
+                    at = 7 * side
+                    weight = (PENALTY * UNIT_LENGTH) * fill_in[side]
+                    for r in range(3):
+                        other = face_in[step, side, r * 64 : r * 64 + 64, :].astype(F32).reshape(8, 8, LANES)
+                        extra = weight * (other - slab(cur, r, at))
+                        put_slab(part, r, at, slab(part, r, at) + extra)
 
         with phase("m_load"):
             loads[0].wait()
@@ -419,7 +431,6 @@
         def _():
             send(fill_send, fill_in.at[1], sent.at[7 + 0], got.at[8 + 1], grp, blk - 1)
 
-        send_faces(0)
         loads[1].wait()
         for step in range(STEPS):
             with phase("m_elastic"):
@@ -427,25 +438,12 @@
             if step == 0:
                 with phase("m_send_dil"):
                     send_taken(0, 0, 8)
+            if step == 0:
+                send_faces(0)
             if step > 0:
                 send_faces(step)
-            with phase("m_faces"):
-                for side, present in ((0, has_below), (1, has_above)):
-
-                    @pl.when(present)
-                    def _():
-                        wait_all(face_in.at[step, side], got.at[4 + 2 * step + side])
-                        wait_all(face_in.at[step, side], sent.at[3 + 2 * step + side])
-                        if step == 0:
-                            wait_all(fill_send, got.at[8 + side])
-                            wait_all(fill_send, sent.at[7 + side])
-
-                    at = 7 * side
-                    weight = (PENALTY * UNIT_LENGTH) * fill_in[side]
-                    for r in range(3):
-                        other = face_in[step, side, pl.ds(r * 64, 64), :].reshape(8, 8, LANES)
-                        extra = weight * (other - slab(cur, r, at))
-                        put_slab(part, r, at, slab(part, r, at) + extra)
+            if step + 1 < STEPS:
+                meet_faces(step)
             for at, (first, last) in enumerate(PRESSURE_SPANS[step]):
                 lanes = slice(first * 64, last * 64)
                 with phase("m_wait_press"):
@@ -464,6 +462,8 @@
                 with phase("m_swell"):
                     for i in range(first, last):
                         swell(i, 0)
+                if step + 1 == STEPS:
+                    meet_faces(step)
                 with phase("m_advance"):
                     for i in range(max(first - 1, 0), last - 1 if last < 8 else 8):
                         advance(i, 0)
@@ -626,31 +626,29 @@
 
             lax.fori_loop(0, 8, one_i, 0)
 
-        def send_pressure(step):
-            for at, (first, last) in enumerate(PRESSURE_SPANS[step]):
-                wide = slice(first * 64, last * 64)
-                lanes = pl.ds(first * 64, (last - first) * 64)
-                for g in range(n_mech):
-                    taken = lax.dot_general(
-                        hits[g * n_blk * CAP : (g + 1) * n_blk * CAP, :],
-                        pi_rows[wide, :],
-                        (((1,), (1,)), ((), ())),
-                        preferred_element_type=F32,
-                    )
-                    press_send[step, g * n_blk : (g + 1) * n_blk, :, wide] = taken.reshape(
-                        n_blk, CAP, (last - first) * 64
-                    ).astype(BF16)
-
-                    for shift in far_first(g < 2):
-                        c = columns[shift]
-                        send(
-                            press_send.at[step, g * n_blk + c, :, lanes],
-                            press_in.at[step, blk, :, lanes],
-                            sent.at[step],
-                            got.at[3 * step + at],
-                            g,
-                            c,
-                        )
+        def send_pressure(step, span, g):
+            first, last = PRESSURE_SPANS[step][span]
+            wide = slice(first * 64, last * 64)
+            lanes = pl.ds(first * 64, (last - first) * 64)
+            taken = lax.dot_general(
+                hits[g * n_blk * CAP : (g + 1) * n_blk * CAP, :],
+                pi_rows[wide, :],
+                (((1,), (1,)), ((), ())),
+                preferred_element_type=F32,
+            )
+            press_send[step, g * n_blk : (g + 1) * n_blk, :, wide] = taken.reshape(
+                n_blk, CAP, (last - first) * 64
+            ).astype(BF16)
+            for shift in far_first(g < 2):
+                c = columns[shift]
+                send(
+                    press_send.at[step, g * n_blk + c, :, lanes],
+                    press_in.at[step, blk, :, lanes],
+                    sent.at[step],
+                    got.at[3 * step + span],
+                    g,
+                    c,
+                )
 
         with phase("s_pi"):
             make_pressure(0)
@@ -672,23 +670,35 @@
 
         with phase("s_wait_oct"):
             wait_all(oct_in, got.at[0])
-        with phase("s_hits"):
-            spread = (n_mech * n_blk, CAP, LANES)
-            one_code = jnp.where(
-                iota(spread, 1) == iota(spread, 2), jnp.broadcast_to(oct_in[...], spread), 0.0
-            )
+        def find_hits(g):
+            spread = (n_blk, CAP, LANES)
+            codes = jnp.broadcast_to(oct_in[g * n_blk : (g + 1) * n_blk], spread)
+            one_code = jnp.where(iota(spread, 1) == iota(spread, 2), codes, 0.0)
             wanted = jnp.dot(
-                one_code.reshape(n_mech * n_blk * CAP, LANES).astype(BF16),
+                one_code.reshape(n_blk * CAP, LANES).astype(BF16),
                 jnp.ones((LANES, LANES), BF16),
                 preferred_element_type=F32,
             )
             lane = iota(wanted.shape, 1)
+            rows = slice(g * n_blk * CAP, (g + 1) * n_blk * CAP)
             for t in range(4):
                 at_octant = (lane + t * DEPTH_OCTANTS).astype(F32) - CODE_SHIFT
-                mine = (wanted == at_octant) & (lane < DEPTH_OCTANTS)
-                hits[:, t * LANES : (t + 1) * LANES] = flag(mine, BF16)
+                found = (wanted == at_octant) & (lane < DEPTH_OCTANTS)
+                hits[rows, t * LANES : (t + 1) * LANES] = flag(found, BF16)
+
         with phase("s_send_press"):
-            send_pressure(0)
+            find_hits(0)
+            send_pressure(0, 0, 0)
+            find_hits(1)
+            send_pressure(0, 0, 1)
+            find_hits(2)
+            send_pressure(0, 0, 2)
+            send_pressure(0, 1, 0)
+            send_pressure(0, 1, 1)
+            send_pressure(0, 1, 2)
+            send_pressure(0, 2, 0)
+            send_pressure(0, 2, 1)
+            send_pressure(0, 2, 2)
         @pl.when(jnp.logical_not(has_below))
         def _():
             diff[0:LAYER, :] = jnp.zeros((LAYER, LANES), F32)
@@ -707,7 +717,8 @@
                 with phase("s_pi"):
                     make_pressure(step)
                 with phase("s_send_press"):
-                    send_pressure(step)
+                    for g in range(n_mech):
+                        send_pressure(step, 0, g)
             for g in (2, 0, 1):
                 span = slice(g * n_blk, (g + 1) * n_blk)
                 rows = slice(g * n_blk * CAP, (g + 1) * n_blk * CAP)
@@ -827,7 +838,8 @@
             vmem((NODES, LANES), F32),
             vmem((STEPS, n_blk, CAP, NODES), BF16),
             vmem((NODES, LANES), F32),
-            vmem((STEPS, 2, 192, LANES), F32),
+            vmem((STEPS, 2, 192, LANES), BF16),
+            vmem((2, 192, LANES), BF16),
             vmem((2, 8, LANES), F32),
             vmem((8, LANES), F32),
             vmem(whole, F32),

time: 37.5 us -> 37.1 us (0.989); the launches traced: 37 us -> 37 us
  no operation moved by 1% of the time
where the time goes in v4:
time: 37.1 us; the launch traced here: 37 us
  Pallas kernels  36.1 us (97%)
  local copies, waits for them, and re-layouts  0.88 us (2%)
    pallas_call x1, Pallas kernels, shards(): call(*(pltpu.with_memory_space_constraint(x, pltpu.HBM) for x in operands))  36.1 us
    unnamed x1, local copies, waits for them, and re-layouts  0.88 us

profile of v4, /device:TPU:49, one launch (start us, length us, event | category | flops | bytes accessed | tf_op | source)
XLA Modules:
  0.0 37.0 jit_solution(12540293921245974707)
XLA Ops:
  0.0 36.1 %shard_map.55 = f32[1536,128]{1,0:T(8,128)S(1)} custom-call(f32[1536,128]{1,0:T(8,128)} %bitcast.7, f32[1536,128]{1,0:T(8,128)} %bitcast.8, s32[1,128]{1,0:T(1,128)} %bitcast.9, s32[1,128]{1,0:T(1,128)} %bitcast.10, s32[1,128]{1,0:T(1,128)} %bitcast.11), custom_call_target="tpu_custom_call" | custom-call | tf_op jit(solution)/shard_map/pallas_call | solution.py:880
  36.1 0.9 %copy.7 = f32[1,3,512,128]{3,2,1,0:T(8,128)} copy(f32[1,3,512,128]{3,2,1,0:T(8,128)S(1)} %bitcast.6) | data formatting | bytes 1572864

commit v5 on v4

--- a/solution.py
+++ b/solution.py
@@ -71,16 +71,19 @@
     ref[pl.ds(aligned(r * 512 + i * 64, 64), 64), :] = value.reshape(64, LANES)
 
 
-def along_j(s):
-    return jnp.concatenate([s[1:2] - s[0:1], 0.5 * (s[2:] - s[:-2]), s[7:8] - s[6:7]], axis=0)
-
-
-def along_k(s):
+def along_j(s, scale=1.0):
+    first, last = s[1:2] - s[0:1], s[7:8] - s[6:7]
+    if scale != 1.0:
+        first, last = scale * first, scale * last
+    return jnp.concatenate([first, (0.5 * scale) * (s[2:] - s[:-2]), last], axis=0)
+
+
+def along_k(s, scale=1.0):
     k = iota(s.shape, 1)
     edge = (k == 0) | (k == 7)
     upper = jnp.where(k == 7, s, pltpu.roll(s, 7, 1))
     lower = jnp.where(k == 0, s, pltpu.roll(s, 1, 1))
-    return (upper - lower) * jnp.where(edge, 1.0, 0.5)
+    return (upper - lower) * jnp.where(edge, scale, 0.5 * scale)
 
 
 def i_span(i):
@@ -97,8 +100,8 @@
         s = slab(cur, r, i)
         row = [
             (slab(cur, r, above) - slab(cur, r, below)) * (UNIT_LENGTH * scale),
-            along_j(s) * UNIT_LENGTH,
-            along_k(s) * UNIT_LENGTH,
+            along_j(s, UNIT_LENGTH),
+            along_k(s, UNIT_LENGTH),
         ]
         row[r] = row[r] + 1.0
         grads.append(row)
@@ -286,6 +289,8 @@
             for step in range(STEPS):
                 face_in[step, 1] = jnp.zeros((192, LANES), BF16)
 
+        swelling = filled * DILATION_SCALE
+
         def dilate(i, carry):
             f = gradients(cur, i)
             det = (
@@ -293,7 +298,7 @@
                 - f[0][1] * (f[1][0] * f[2][2] - f[1][2] * f[2][0])
                 + f[0][2] * (f[1][0] * f[2][1] - f[1][1] * f[2][0])
             )
-            change = (det - 1.0) * filled * DILATION_SCALE
+            change = (det - 1.0) * swelling
             for j in range(8):
                 dil_rows[pl.ds(i * 64 + j, 8, stride=8), :] = change[j]
             return carry

time: 37.1 us -> 37 us (level)
  no operation moved by 1% of the time
where the time goes in v5:
time: 37 us; the launch traced here: 36.9 us
  Pallas kernels  36 us (97%)
  local copies, waits for them, and re-layouts  0.88 us (2%)
    pallas_call x1, Pallas kernels, shards(): call(*(pltpu.with_memory_space_constraint(x, pltpu.HBM) for x in operands))  36 us
    unnamed x1, local copies, waits for them, and re-layouts  0.88 us

profile of v5, /device:TPU:49, one launch (start us, length us, event | category | flops | bytes accessed | tf_op | source)
XLA Modules:
  0.0 36.9 jit_solution(16309914403984734510)
XLA Ops:
  0.0 36.0 %shard_map.55 = f32[1536,128]{1,0:T(8,128)S(1)} custom-call(f32[1536,128]{1,0:T(8,128)} %bitcast.7, f32[1536,128]{1,0:T(8,128)} %bitcast.8, s32[1,128]{1,0:T(1,128)} %bitcast.9, s32[1,128]{1,0:T(1,128)} %bitcast.10, s32[1,128]{1,0:T(1,128)} %bitcast.11), custom_call_target="tpu_custom_call" | custom-call | tf_op jit(solution)/shard_map/pallas_call | solution.py:885
  36.0 0.9 %copy.7 = f32[1,3,512,128]{3,2,1,0:T(8,128)} copy(f32[1,3,512,128]{3,2,1,0:T(8,128)S(1)} %bitcast.6) | data formatting | bytes 1572864

commit v6 on v5

--- a/solution.py
+++ b/solution.py
@@ -24,7 +24,7 @@
 LANES = 128
 NODES = 512
 CAP = 8
-HALO_PIECE = 64
+HALO_PIECE = 32
 DEPTH_OCTANTS = 96
 CODE_SHIFT = 191.0
 EMPTY_CODE = -1000.0

time: 37 us -> 37 us (level)
  no operation moved by 1% of the time
where the time goes in v6:
time: 37 us; the launch traced here: 36.9 us
  Pallas kernels  36 us (97%)
  local copies, waits for them, and re-layouts  0.88 us (2%)
    pallas_call x1, Pallas kernels, shards(): call(*(pltpu.with_memory_space_constraint(x, pltpu.HBM) for x in operands))  36 us
    unnamed x1, local copies, waits for them, and re-layouts  0.88 us

profile of v6, /device:TPU:49, one launch (start us, length us, event | category | flops | bytes accessed | tf_op | source)
XLA Modules:
  0.0 36.9 jit_solution(3826143274069761858)
XLA Ops:
  0.0 36.0 %shard_map.55 = f32[1536,128]{1,0:T(8,128)S(1)} custom-call(f32[1536,128]{1,0:T(8,128)} %bitcast.7, f32[1536,128]{1,0:T(8,128)} %bitcast.8, s32[1,128]{1,0:T(1,128)} %bitcast.9, s32[1,128]{1,0:T(1,128)} %bitcast.10, s32[1,128]{1,0:T(1,128)} %bitcast.11), custom_call_target="tpu_custom_call" | custom-call | tf_op jit(solution)/shard_map/pallas_call | solution.py:885
  36.0 0.9 %copy.7 = f32[1,3,512,128]{3,2,1,0:T(8,128)} copy(f32[1,3,512,128]{3,2,1,0:T(8,128)S(1)} %bitcast.6) | data formatting | bytes 1572864
